TPU v7x, 256 devices: a whole 4x4x8 slice. The times are simulated.
256 devices in a mesh: dp: 4 (over z_lo), member: 2 (over z_hi), space: 32 (over x, y, core).
Axes of the slice: x: 4, y: 4, z: 8 (z_hi: 2, z_lo: 4; z = z_hi * 4 + z_lo), core: 2. Of those that a mesh axis runs over, the one named last changes fastest.
Arguments:
- grid_in: bfloat16 [4, 84, 16384], P('dp', None, 'space'), may hold values from -6 to 6
- target: bfloat16 [4, 84, 16384], P('dp', None, 'space'), may hold values from -6 to 6
- noise: float32 [4, 8, 32], P('dp', 'member'), may hold values from -6 to 6
- neighbours: int32 [64, 3], P('space'), may hold values from 0 to 63, as said below
- enc_index: int32 [4096, 4], P('space'), may hold values from 0 to 16383, as said below
- dec_index: int32 [16384, 3], P('space'), may hold values from 0 to 4095, as said below
- w_in: bfloat16 [84, 768], replicated, may hold values from -0.625 to 0.625
- w_gamma: float32 [32, 768], replicated, may hold values from -0.6 to 0.6
- w_beta: float32 [32, 768], replicated, may hold values from -0.6 to 0.6
- w_qkv: bfloat16 [768, 2304], replicated, may hold values from -60 to 60
- w_o: bfloat16 [768, 768], replicated, may hold values from -0.8984375 to 0.8984375
- readout_matrix: bfloat16 [84, 768], replicated, may hold values from -0.21875 to 0.21875
Outputs:
- predicted_states: bfloat16 [4, 8, 84, 16384], P('dp', 'member', None, 'space')
- objective_mean: float32 [], replicated
- unit_descent_slope: float32 [84, 768], replicated
Inputs may be any that keep to these rules, and one draw needn't show every extreme that they name: `neighbours`: row w lists three different windows other than w whose ids differ from w by 1 or 2, counted around the 64 windows. `enc_index`: rows j * 128 to (j + 1) * 128 - 1 name only grid points j * 512 to (j + 1) * 512 - 1. `dec_index`: rows j * 512 to (j + 1) * 512 - 1 name only tokens j * 128 to (j + 1) * 128 - 1.
All inputs are finite; a program needn't handle non-finite values.
Results may differ from a plain program's by a relative error of at most 0.0065.
The roundings to bfloat16 on the way count: a program that leaves them out, or rounds other values in their place, can miss the bound.
Values may be sent and summed in bfloat16 or wider, within the bound.
No kernel may reach another device: no remote copies, remote signals or barrier semaphores. Data moves between devices by JAX's collectives and lax.ppermute only.
A program may use at most 128 MiB of HBM per device.

v0:
```python
import functools

import jax
import jax.numpy as jnp
from jax import lax
from jax.experimental import pallas as pl
from jax.experimental.pallas import tpu as pltpu
from jax.sharding import PartitionSpec as P

HEADS = 12
HD = 64
WIN = 64
K_ENC = 4
K_DEC = 3
EPSILON = 1e-06
LANES = 128
GROUP = 4
LOG2E = 1.4426950408889634

F32 = jnp.float32
BF16 = jnp.bfloat16

VMEM = pl.BlockSpec(memory_space=pltpu.VMEM)
SMEM = pl.BlockSpec(memory_space=pltpu.SMEM)
NT = (((1,), (1,)), ((), ()))


def dot(a, b):
    return jnp.dot(a, b, preferred_element_type=F32)


def dot_nt(a, b):
    return lax.dot_general(a, b, NT, preferred_element_type=F32)


def call(kernel, outs, args, smem=(), scratch=(), limit=24, work=0):
    many = isinstance(outs, list)
    kept = [
        a if i in smem else pltpu.with_memory_space_constraint(a, pltpu.VMEM) for i, a in enumerate(args)
    ]
    return pl.pallas_call(
        kernel,
        out_shape=outs,
        in_specs=[SMEM if i in smem else VMEM for i in range(len(args))],
        out_specs=[VMEM] * len(outs) if many else VMEM,
        scratch_shapes=list(scratch),
        compiler_params=pltpu.CompilerParams(vmem_limit_bytes=limit << 20),
        cost_estimate=pl.CostEstimate(flops=work, transcendentals=0, bytes_accessed=work // 100),
    )(*kept)


def counts_of(index_rows, targets):
    many = index_rows.shape[1]
    local = lax.rem(index_rows, jnp.int32(targets))
    positions = lax.broadcasted_iota(jnp.int32, (targets, many), 0)
    counts = (local[0:1, :] == positions).astype(F32)
    for row in range(1, index_rows.shape[0]):
        counts = counts + (local[row : row + 1, :] == positions).astype(F32)
    return counts


def pool_kernel(enc_ref, grid_ref, pooled_ref):
    counts = counts_of(enc_ref[...], grid_ref.shape[1]).astype(BF16)
    pooled_ref[...] = dot(grid_ref[...], counts) * (1.0 / K_ENC)


def states_of(pooled, w_in):
    values = pooled.T
    high = values.astype(BF16)
    rest = values - high.astype(F32)
    mid = rest.astype(BF16)
    low = (rest - mid.astype(F32)).astype(BF16)
    return dot(high, w_in) + (dot(mid, w_in) + dot(low, w_in))


def normed_of(states):
    centre = states - jnp.mean(states, axis=-1, keepdims=True)
    spread = jnp.mean(centre * centre, axis=-1, keepdims=True)
    return centre / jnp.sqrt(spread + EPSILON)


def own_kernel(
    pooled_ref,
    w_in_ref,
    noise_ref,
    w_gamma_ref,
    w_beta_ref,
    w_qkv_ref,
    dec_ref,
    states_ref,
    gain_ref,
    shift_ref,
    project_ref,
    counts_ref,
    inputs_ref,
):
    tok, d = states_ref.shape
    members = noise_ref.shape[0]
    gain = 1.0 + jnp.dot(noise_ref[...], w_gamma_ref[...], precision=lax.Precision.HIGHEST)
    shift = jnp.dot(noise_ref[...], w_beta_ref[...], precision=lax.Precision.HIGHEST)
    gain_ref[...] = gain
    shift_ref[...] = shift
    states = states_of(pooled_ref[...], w_in_ref[...])
    states_ref[...] = states
    normed = normed_of(states)
    for m in range(members):
        inputs_ref[m * tok : (m + 1) * tok, :] = (normed * gain[m : m + 1] + shift[m : m + 1]).astype(BF16)
    for c in range(3):
        part = dot(inputs_ref[...], w_qkv_ref[:, c * d : (c + 1) * d])
        project_ref[:, c * d : (c + 1) * d] = part.astype(BF16)
    counts = counts_of(dec_ref[...], tok).T.astype(BF16)
    counts_ref[:, :tok] = counts
    counts_ref[:, tok:] = counts


def members_kernel(
    begin,
    nbr_ref,
    pair_ref,
    next_ref,
    w_in_ref,
    gain_ref,
    shift_ref,
    project_ref,
    states_ref,
    counts_ref,
    grid_ref,
    w_qkv_ref,
    w_o_ref,
    readout_ref,
    x_ref,
    feat_ref,
    *refs,
):
    edge_ref, kv_ref, att_ref, upd_ref = refs[-4:]
    tok, d = states_ref.shape
    members = x_ref.shape[0]
    wins = tok // WIN
    wide = GROUP * HD
    windows = wins * lax.axis_size("space")
    first = lax.axis_index("space") * wins
    odd = lax.rem(lax.axis_index("space"), 2) == 1
    for slot in range(2):
        if begin == 0:
            pooled = jnp.where(odd == (slot == 0), pair_ref[...], next_ref[...])
            normed = normed_of(states_of(pooled, w_in_ref[...]))
            refs[0][slot * tok : (slot + 1) * tok, :] = normed
        else:
            normed = pair_ref[slot * tok : (slot + 1) * tok, :]
        for m in range(members):
            row = (2 * m + slot) * tok
            k = begin + m
            edge_ref[row : row + tok, :] = (
                normed * gain_ref[k : k + 1, :] + shift_ref[k : k + 1, :]
            ).astype(BF16)
    for c in range(2):
        lo = c * d
        part = dot(edge_ref[...], w_qkv_ref[:, d + lo : d + lo + d]).astype(BF16)
        for m in range(members):
            kv_ref[m, :tok, lo : lo + d] = part[2 * m * tok : (2 * m + 1) * tok]
            kv_ref[m, tok : 2 * tok, lo : lo + d] = project_ref[
                (begin + m) * tok : (begin + m + 1) * tok, d + lo : d + lo + d
            ]
            kv_ref[m, 2 * tok :, lo : lo + d] = part[(2 * m + 1) * tok : (2 * m + 2) * tok]
    head_of = lax.broadcasted_iota(jnp.int32, (WIN, wide), 1) // HD

    def attend(m, carry):
        for w in range(wins):
            starts = [(wins + w) * WIN]
            for j in range(nbr_ref.shape[1]):
                reach = lax.rem(nbr_ref[w, j] - first - w + 2 + windows, windows) + w
                starts.append(pl.multiple_of(reach * WIN, WIN))
            row = pl.multiple_of(m * tok + w * WIN, WIN)
            for g in range(HEADS // GROUP):
                lo = g * wide
                q = project_ref[pl.ds(begin * tok + row, WIN), lo : lo + wide]
                zero = jnp.zeros_like(q)
                spread = jnp.concatenate([jnp.where(head_of == h, q, zero) for h in range(GROUP)], axis=0)
                keys = jnp.concatenate([kv_ref[m, pl.ds(s, WIN), lo : lo + wide] for s in starts], axis=0)
                values = jnp.concatenate(
                    [kv_ref[m, pl.ds(s, WIN), d + lo : d + lo + wide] for s in starts], axis=0
                )
                scores = dot_nt(spread, keys) * (HD ** (-0.5) * LOG2E)
                top = jnp.max(scores, axis=-1, keepdims=True)
                weights = jnp.exp2(scores - top)
                weights = weights * (1.0 / jnp.sum(weights, axis=-1, keepdims=True))
                mixed = dot(weights.astype(BF16), values)
                out = mixed[:WIN]
                for h in range(1, GROUP):
                    out = jnp.where(head_of == h, mixed[h * WIN : (h + 1) * WIN], out)
                att_ref[pl.ds(row, WIN), lo : lo + wide] = out.astype(BF16)
        return carry

    lax.fori_loop(0, members, attend, 0)
    mixed = dot(att_ref[...], w_o_ref[...])
    for m in range(members):
        updated = states_ref[...] + mixed[m * tok : (m + 1) * tok]
        high = updated.astype(BF16)
        upd_ref[m, :tok, :] = high
        upd_ref[m, tok:, :] = (updated - high.astype(F32)).astype(BF16)

    def decode(m, carry):
        features = (dot(counts_ref[...], upd_ref[m]) / K_DEC).astype(BF16)
        feat_ref[m] = features
        x_ref[m] = (grid_ref[...].astype(F32) + dot_nt(readout_ref[...], features)).astype(BF16)
        return carry

    lax.fori_loop(0, members, decode, 0)


def pair_list(own, other):
    pairs = [(i, j) for i in range(own) for j in range(i + 1, own)]
    cross = [(i, own + j) for i in range(own) for j in range(other)]
    return pairs, cross


def stats_kernel(members, target_ref, *refs):
    out_ref = refs[-1]
    xs = [r[i].astype(F32) for r in refs[:-1] for i in range(r.shape[0])]
    truth = target_ref[...].astype(F32)
    pairs, cross = pair_list(members, len(xs) - members)
    rows = []

    def lane_sums(diff):
        col = jnp.sum(diff * diff, axis=0, keepdims=True)
        total = col[:, :LANES]
        for c in range(1, col.shape[1] // LANES):
            total = total + col[:, c * LANES : (c + 1) * LANES]
        return total

    for i in range(members):
        rows.append(lane_sums(xs[i] - truth))
    for i, j in pairs + cross:
        rows.append(lane_sums(xs[i] - xs[j]))
    row_id = lax.broadcasted_iota(jnp.int32, (32, LANES), 0)
    lane_id = lax.broadcasted_iota(jnp.int32, (32, LANES), 1)
    table = jnp.zeros((32, LANES), F32)
    for k, row in enumerate(rows):
        table = jnp.where(row_id == k, row, table)
    sums = jnp.sum(table, axis=1, keepdims=True)
    line = jnp.sum(jnp.where(row_id == lane_id, sums, 0.0), axis=0, keepdims=True)
    out_ref[...] = jnp.broadcast_to(line[None], out_ref.shape)


def slope_kernel(
    members, members_all, stat_ref, target_ref, *refs
):
    parts = (len(refs) - 4) // 3
    pred_ref, grad_ref, score_ref, pack_ref = refs[-4:]
    xs = [r[i] for r in refs[: 2 * parts] for i in range(r.shape[0])]
    feats = [r.at[i] for r in refs[2 * parts : 3 * parts] for i in range(r.shape[0])]
    xf = [x.astype(F32) for x in xs]
    truth = target_ref[...].astype(F32)
    pairs, cross = pair_list(members, members)
    total = jnp.sum(stat_ref[...].reshape(stat_ref.shape[0], LANES), axis=0, keepdims=True)
    dist = jnp.sqrt(total + EPSILON)
    lane = lax.broadcasted_iota(jnp.int32, (1, LANES), 1)
    first_cross = members + len(pairs)
    end = first_cross + len(cross)
    m = float(members_all)
    share = jnp.where(
        lane < members,
        1.0 / m,
        jnp.where(lane < first_cross, -1.0 / (m * m), jnp.where(lane < end, -0.5 / (m * m), 0.0)),
    )
    score = jnp.sum(dist * share, axis=1, keepdims=True)
    score_ref[...] = jnp.broadcast_to(score, score_ref.shape)
    pull = 1.0 / (jnp.where(lane < members, m, m * m) * dist)
    coef = {}
    for k, (i, j) in enumerate(pairs + cross):
        value = pull[:, members + k : members + k + 1]
        coef[i, j] = value
        coef[j, i] = value
    acc = None
    for i in range(members):
        pred_ref[i] = xs[i]
        slope = pull[:, i : i + 1] * (xf[i] - truth)
        for j in range(2 * members):
            if j != i:
                slope = slope + coef[i, j] * (xf[j] - xf[i])
        part = dot(slope.astype(BF16), feats[i][...])
        acc = part if acc is None else acc + part
    v, d = acc.shape
    pack_ref[...] = jnp.zeros_like(pack_ref)
    for c in range(d // LANES):
        pack_ref[c * v : (c + 1) * v, :] = acc[:, c * LANES : (c + 1) * LANES]
    grad_ref[...] = pack_ref[...].astype(BF16).reshape(grad_ref.shape)


def share_kernel(recv_ref, score_ref, out_ref):
    total = jnp.sum(recv_ref[...].astype(F32), axis=0)
    both = jnp.concatenate([total, score_ref[...]], axis=0)
    out_ref[...] = jnp.broadcast_to(both[None], out_ref.shape)


def spread_kernel(scale, recv_ref, out_ref, score_ref):
    rows = out_ref.shape[1]
    total = jnp.sum(recv_ref[...], axis=0)
    out_ref[...] = jnp.broadcast_to(total[:rows][None], out_ref.shape)
    score_ref[...] = total[rows:] * scale


def final_kernel(recv_ref, out_ref, pack_ref):
    v, d = out_ref.shape
    pack_ref[...] = recv_ref[...].reshape(pack_ref.shape)
    grad = pack_ref[...]
    square = jnp.sum(jnp.sum(grad * grad, axis=0, keepdims=True), axis=1, keepdims=True)
    scale = 1.0 / jnp.sqrt(square / (v * d) + EPSILON)
    for c in range(d // LANES):
        out_ref[:, c * LANES : (c + 1) * LANES] = pack_ref[c * v : (c + 1) * v, :] * scale


def exchange(blocks, axis):
    return lax.all_to_all(blocks, axis, split_axis=0, concat_axis=0, tiled=True)


def step(
    grid_in,
    target,
    noise,
    neighbours,
    enc_index,
    dec_index,
    w_in,
    w_gamma,
    w_beta,
    w_qkv,
    w_o,
    readout_matrix,
):
    tok = enc_index.shape[0]
    points = dec_index.shape[0]
    d = w_o.shape[0]
    members = noise.shape[1]
    v = grid_in.shape[1]
    space = lax.axis_size("space")
    grid = grid_in[0]
    truth = target[0]

    pooled = call(pool_kernel, pltpu.VMEM((v, tok), F32), (enc_index.T, grid), work=4 * 10**9)
    pairs = [(i, i ^ 1) for i in range(space)]
    nexts = [(i, (i + 1 if i % 2 else i - 1) % space) for i in range(space)]
    from_pair = lax.ppermute(pooled, "space", pairs)
    from_next = lax.ppermute(pooled, "space", nexts)
    states, gain, shift, project, counts = call(
        own_kernel,
        [
            pltpu.VMEM((tok, d), F32),
            pltpu.VMEM((members, d), F32),
            pltpu.VMEM((members, d), F32),
            pltpu.VMEM((members * tok, 3 * d), BF16),
            pltpu.VMEM((points, 2 * tok), BF16),
        ],
        (pooled, w_in, noise[0], w_gamma, w_beta, w_qkv, dec_index.T),
        scratch=(pltpu.VMEM((members * tok, d), BF16),),
        work=4 * 10**9,
    )
    own, other, feats = [], [], []
    halo = (from_pair, from_next)
    some = members // 2
    for begin in range(0, members, some):
        outs = [pltpu.VMEM((some, v, points), BF16), pltpu.VMEM((some, points, d), BF16)]
        if begin == 0:
            outs.append(pltpu.VMEM((2 * tok, d), F32))
        got = call(
            functools.partial(members_kernel, begin),
            outs,
            (
                neighbours,
                *halo,
                w_in,
                gain,
                shift,
                project,
                states,
                counts,
                grid,
                w_qkv,
                w_o,
                readout_matrix,
            ),
            smem=(0,),
            scratch=(
                pltpu.VMEM((2 * some * tok, d), BF16),
                pltpu.VMEM((some, 3 * tok, 2 * d), BF16),
                pltpu.VMEM((some * tok, d), BF16),
                pltpu.VMEM((some, 2 * tok, d), BF16),
            ),
            work=8 * 10**9,
        )
        if begin == 0:
            halo = (got[2], from_next)
        own.append(got[0])
        feats.append(got[1])
        other.append(lax.ppermute(got[0], "member", [(0, 1), (1, 0)]))
    members_all = members * lax.axis_size("member")
    stats = call(
        functools.partial(stats_kernel, members),
        pltpu.VMEM((space, 1, LANES), F32),
        (truth, *own, *other),
        work=10**9,
    )
    stats = exchange(stats, "space")
    rows = -(-v * d // (LANES * space * 8)) * 8
    pred, grad, score = call(
        functools.partial(slope_kernel, members, members_all),
        [
            jax.ShapeDtypeStruct((members, v, points), BF16),
            pltpu.VMEM((space, rows, LANES), BF16),
            pltpu.VMEM((8, LANES), F32),
        ],
        (stats, truth, *own, *other, *feats),
        scratch=(pltpu.VMEM((space * rows, LANES), F32),),
    )
    grad = exchange(grad, "space")
    peers = lax.axis_size("dp") * lax.axis_size("member")
    share = call(share_kernel, pltpu.VMEM((peers, rows + 8, LANES), F32), (grad, score))
    share = exchange(share, ("dp", "member"))
    scale = 1.0 / (lax.axis_size("dp") * (v * points * space) ** 0.5)
    spread, objective = call(
        functools.partial(spread_kernel, scale),
        [pltpu.VMEM((space, rows, LANES), F32), pltpu.VMEM((8, LANES), F32)],
        (share,),
    )
    spread = exchange(spread, "space")
    unit = call(
        final_kernel,
        jax.ShapeDtypeStruct((v, d), F32),
        (spread,),
        scratch=(pltpu.VMEM((space * rows, LANES), F32),),
    )
    return (pred[None], objective[0, 0], unit)


def solution(mesh):
    in_specs = (
        P("dp", None, "space"),
        P("dp", None, "space"),
        P("dp", "member", None),
        P("space", None),
        P("space", None),
        P("space", None),
        P(),
        P(),
        P(),
        P(),
        P(),
        P(),
    )
    out_specs = (P("dp", "member", None, "space"), P(), P())
    return jax.shard_map(step, mesh=mesh, in_specs=in_specs, out_specs=out_specs, check_vma=False)
```

profile of v0, /device:TPU:1, one launch (start us, length us, event | category | flops | bytes accessed | tf_op | source)
XLA Modules:
  0.0 102.4 jit_solution(5830090095347842535)
XLA Ops:
  0.6 0.0 copy-start.7
  0.6 0.9 copy-done.7
  1.5 0.7 copy-done.10
  2.2 0.3 shard_map.139.pooled_ref
  2.5 2.8 %collective-permute-start.1 = (f32[84,128]{1,0:T(8,128)S(1)}, f32[84,128]{1,0:T(8,128)S(1)}, u32[]{:S(2)}, u32[]{:S(2)}) collective-permute-start(f32[84,128]{1,0:T(8,128)S(1)} %shard_map.139.pooled_ref), channel_id=1, source_target_pairs={{0,31},{1,2},{2,1},{3,4},{4,3},{5,6},{6,5},{7,8},{8,7},{9,10},{10,... | collective-permute-start | bytes 129032 | tf_op jit(solution)/shard_map/ppermute | solution.py:344
  5.3 3.5 %collective-permute-start = (f32[84,128]{1,0:T(8,128)S(1)}, f32[84,128]{1,0:T(8,128)S(1)}, u32[]{:S(2)}, u32[]{:S(2)}) collective-permute-start(f32[84,128]{1,0:T(8,128)S(1)} %shard_map.139.pooled_ref), channel_id=1, source_target_pairs={{0,1},{1,0},{2,3},{3,2},{4,5},{5,4},{6,7},{7,6},{8,9},{9,8},{10,11... | collective-permute-start | bytes 129032 | tf_op jit(solution)/shard_map/ppermute | solution.py:343
  8.7 0.0 copy-done.6
  8.8 0.0 copy-start.2
  8.8 0.0 copy-start.4
  8.8 0.0 copy-start.8
  8.8 0.0 copy-start.12
  8.8 2.7 %shard_map.140 = (f32[128,768]{1,0:T(8,128)S(1)}, f32[4,768]{1,0:T(4,128)S(1)}, f32[4,768]{1,0:T(4,128)S(1)}, bf16[512,2304]{1,0:T(8,128)(2,1)S(1)}, bf16[512,256]{1,0:T(8,128)(2,1)S(1)}) custom-call(f32[84,128]{1,0:T(8,128)S(1)} %shard_map.139.pooled_ref, bf16[84,768]{1,0:T(8,128)(2,1)S(1)} %copy-done.3, f32[4,32]{1,0:T(4,128)S(1)} %bitcast.15, ...), custom_call_target="tpu_custom_call" | custom-call | flops 4000000000 | bytes 40000000 | tf_op jit(solution)/shard_map/pallas_call | solution.py:41
  11.5 0.0 collective-permute-done.1.next_ref
  11.5 0.0 collective-permute-done.pair_ref
  11.6 7.2 %shard_map.141 = (bf16[2,84,512]{2,1,0:T(8,128)(2,1)S(1)}, bf16[2,512,768]{2,1,0:T(8,128)(2,1)S(1)}, f32[256,768]{1,0:T(8,128)S(1)}) custom-call(s32[2,3]{1,0:T(2,128)S(1)} %copy-done.12, f32[84,128]{1,0:T(8,128)S(1)} %collective-permute-done.pair_ref, f32[84,128]{1,0:T(8,128)S(1)} %collective-permute-done.1.next_ref, bf16[84,768]{1,0:T(8,128)(2,1)S(1)} %copy-done.3, ...), custom_call_target="tpu_custom_call" | custom-call | flops 8000000000 | bytes 80000000 | tf_op jit(solution)/shard_map/pallas_call | solution.py:41
  18.8 0.0 copy-start
  18.8 6.3 %shard_map.142 = (bf16[2,84,512]{2,1,0:T(8,128)(2,1)S(1)}, bf16[2,512,768]{2,1,0:T(8,128)(2,1)S(1)}) custom-call(s32[2,3]{1,0:T(2,128)S(1)} %copy-done.12, f32[256,768]{1,0:T(8,128)S(1)} %get-tuple-element.24.pair_ref, f32[84,128]{1,0:T(8,128)S(1)} %collective-permute-done.1.next_ref, bf16[84,768]{1,0:T(8,128)(2,1)S(1)} %copy-done.3, ...), custom_call_target="tpu_custom_call" | custom-call | flops 8000000000 | bytes 80000000 | tf_op jit(solution)/shard_map/pallas_call | solution.py:41
  25.1 7.0 %collective-permute-start.3 = (bf16[2,84,512]{2,1,0:T(8,128)(2,1)S(1)}, bf16[2,84,512]{2,1,0:T(8,128)(2,1)S(1)}, u32[]{:S(2)}, u32[]{:S(2)}) collective-permute-start(bf16[2,84,512]{2,1,0:T(8,128)(2,1)S(1)} %get-tuple-element.25.refs_1_), channel_id=1, source_target_pairs={{0,32},{32,0},{1,33},{33,1},{2,34},{34,2},{3,35},{35,3},{4,36},{36... | collective-permute-start | bytes 516104 | tf_op jit(solution)/shard_map/ppermute | solution.py:395
  32.1 0.1 collective-permute-start.2
  32.2 4.8 %collective-permute-done.3.refs_3_ = bf16[2,84,512]{2,1,0:T(8,128)(2,1)S(1)} collective-permute-done((bf16[2,84,512]{2,1,0:T(8,128)(2,1)S(1)}, bf16[2,84,512]{2,1,0:T(8,128)(2,1)S(1)}, u32[]{:S(2)}, u32[]{:S(2)}) %collective-permute-start.3) | collective-permute-done | bytes 172064 | tf_op jit(solution)/shard_map/ppermute | solution.py:395
  37.0 4.8 %collective-permute-done.2.refs_2_ = bf16[2,84,512]{2,1,0:T(8,128)(2,1)S(1)} collective-permute-done((bf16[2,84,512]{2,1,0:T(8,128)(2,1)S(1)}, bf16[2,84,512]{2,1,0:T(8,128)(2,1)S(1)}, u32[]{:S(2)}, u32[]{:S(2)}) %collective-permute-start.2) | collective-permute-done | bytes 172064 | tf_op jit(solution)/shard_map/ppermute | solution.py:395
  41.8 0.8 shard_map.143
  42.6 17.2 %all_to_all.20.stat_ref = f32[32,1,128]{2,1,0:T(1,128)S(1)} all-to-all(f32[32,1,128]{2,1,0:T(1,128)S(1)} %shard_map.143), channel_id=1, replica_groups=mesh['dp'=4,'member'=2,'space'=32] {'space'}, dimensions={0} | all-to-all | bytes 32768 | tf_op jit(solution)/shard_map/all_to_all | solution.py:314
  59.8 1.1 %shard_map.144 = (bf16[4,84,512]{2,1,0:T(8,128)(2,1)S(1)}, bf16[32,16,128]{2,1,0:T(8,128)(2,1)S(1)}, f32[8,128]{1,0:T(8,128)S(1)}) custom-call(f32[32,1,128]{2,1,0:T(1,128)S(1)} %all_to_all.20.stat_ref, bf16[84,512]{1,0:T(8,128)(2,1)S(1)} %bitcast.9, bf16[2,84,512]{2,1,0:T(8,128)(2,1)S(1)} %get-tuple-element.23.refs_0_, ...), custom_call_target="tpu_custom_call" | custom-call | tf_op jit(solution)/shard_map/pallas_call | solution.py:41
  60.9 11.4 %all_to_all.21.recv_ref = bf16[32,16,128]{2,1,0:T(8,128)(2,1)S(1)} all-to-all(bf16[32,16,128]{2,1,0:T(8,128)(2,1)S(1)} %get-tuple-element.29), channel_id=1, replica_groups=mesh['dp'=4,'member'=2,'space'=32] {'space'}, dimensions={0} | all-to-all | bytes 262144 | tf_op jit(solution)/shard_map/all_to_all | solution.py:314
  72.3 14.1 %all_to_all.22.recv_ref = f32[8,24,128]{2,1,0:T(8,128)S(1)} all-to-all(f32[8,24,128]{2,1,0:T(8,128)S(1)} %shard_map.145), channel_id=1, replica_groups=mesh['dp'=4,'member'=2,'space'=32] {'dp','member'}, dimensions={0} | all-to-all | bytes 196608 | tf_op jit(solution)/shard_map/all_to_all | solution.py:314
  86.4 0.7 shard_map.146
  87.1 5.3 %all-to-all-start.3 = ((f32[32,16,128]{2,1,0:T(8,128)}), f32[32,16,128]{2,1,0:T(8,128)S(1)}, u32[]{:S(2)}, u32[]{:S(2)}) async-start(f32[32,16,128]{2,1,0:T(8,128)} %get-tuple-element.32), calls=%async_computation.3 | async-start | bytes 524288 | tf_op jit(solution)/shard_map/all_to_all | solution.py:314
  92.4 0.9 copy.15
  93.3 0.5 slice.3
  93.9 7.7 %all-to-all-done.3.recv_ref = f32[32,16,128]{2,1,0:T(8,128)S(1)} async-done(((f32[32,16,128]{2,1,0:T(8,128)}), f32[32,16,128]{2,1,0:T(8,128)S(1)}, u32[]{:S(2)}, u32[]{:S(2)}) %all-to-all-start.3) | async-done | bytes 262176 | tf_op jit(solution)/shard_map/all_to_all | solution.py:314
  101.5 0.9 shard_map.147
  (18 shorter events, 0.1 us)
Async XLA Ops:
  0.6 0.9 copy-start.7
  1.5 0.7 copy-start.10
  2.2 6.5 %copy-start.1 = (bf16[768,2304]{1,0:T(8,128)(2,1)S(1)}, bf16[768,2304]{1,0:T(8,128)(2,1)}, u32[]{:S(2)}) copy-start(bf16[768,2304]{1,0:T(8,128)(2,1)} %w_qkv_ref.5) | copy-start | bytes 10616836
  2.2 6.5 %copy-start.3 = (bf16[84,768]{1,0:T(8,128)(2,1)S(1)}, bf16[84,768]{1,0:T(8,128)(2,1)}, u32[]{:S(2)}) copy-start(bf16[84,768]{1,0:T(8,128)(2,1)} %w_in_ref.5) | copy-start | bytes 387076
  2.2 6.5 %copy-start.5 = (f32[32,768]{1,0:T(8,128)S(1)}, f32[32,768]{1,0:T(8,128)}, u32[]{:S(2)}) copy-start(f32[32,768]{1,0:T(8,128)} %w_gamma_ref.1) | copy-start | bytes 294916
  2.2 6.5 %copy-start.6 = (f32[32,768]{1,0:T(8,128)S(1)}, f32[32,768]{1,0:T(8,128)}, u32[]{:S(2)}) copy-start(f32[32,768]{1,0:T(8,128)} %w_beta_ref.1) | copy-start | bytes 294916
  2.2 6.5 %copy-start.9 = (s32[512,3]{0,1:T(4,128)S(1)}, s32[512,3]{0,1:T(4,128)}, u32[]{:S(2)}) copy-start(s32[512,3]{0,1:T(4,128)} %param.17) | copy-start | bytes 18436
  2.2 6.5 %copy-start.11 = (f32[1,4,32]{2,1,0:T(4,128)S(1)}, f32[1,4,32]{2,1,0:T(4,128)}, u32[]{:S(2)}) copy-start(f32[1,4,32]{2,1,0:T(4,128)} %param.14) | copy-start | bytes 1540
  2.5 9.0 %collective-permute-start.1 = (f32[84,128]{1,0:T(8,128)S(1)}, f32[84,128]{1,0:T(8,128)S(1)}, u32[]{:S(2)}, u32[]{:S(2)}) collective-permute-start(f32[84,128]{1,0:T(8,128)S(1)} %shard_map.139.pooled_ref), channel_id=1, source_target_pairs={{0,31},{1,2},{2,1},{3,4},{4,3},{5,6},{6,5},{7,8},{8,7},{9,10},{10,... | collective-permute-start | bytes 129032 | tf_op jit(solution)/shard_map/ppermute | solution.py:344
  5.3 6.3 %collective-permute-start = (f32[84,128]{1,0:T(8,128)S(1)}, f32[84,128]{1,0:T(8,128)S(1)}, u32[]{:S(2)}, u32[]{:S(2)}) collective-permute-start(f32[84,128]{1,0:T(8,128)S(1)} %shard_map.139.pooled_ref), channel_id=1, source_target_pairs={{0,1},{1,0},{2,3},{3,2},{4,5},{5,4},{6,7},{7,6},{8,9},{9,8},{10,11... | collective-permute-start | bytes 129032 | tf_op jit(solution)/shard_map/ppermute | solution.py:343
  8.8 2.8 %copy-start.2 = (bf16[768,768]{1,0:T(8,128)(2,1)S(1)}, bf16[768,768]{1,0:T(8,128)(2,1)}, u32[]{:S(2)}) copy-start(bf16[768,768]{1,0:T(8,128)(2,1)} %w_o_ref.3) | copy-start | bytes 3538948
  8.8 2.8 %copy-start.4 = (bf16[84,768]{1,0:T(8,128)(2,1)S(1)}, bf16[84,768]{1,0:T(8,128)(2,1)}, u32[]{:S(2)}) copy-start(bf16[84,768]{1,0:T(8,128)(2,1)} %readout_ref.3) | copy-start | bytes 387076
  8.8 2.8 %copy-start.8 = (bf16[1,84,512]{2,1,0:T(8,128)(2,1)S(1)}, bf16[1,84,512]{2,1,0:T(8,128)(2,1)}, u32[]{:S(2)}) copy-start(bf16[1,84,512]{2,1,0:T(8,128)(2,1)} %param.12) | copy-start | bytes 258052
  8.8 2.8 %copy-start.12 = (s32[2,3]{1,0:T(2,128)S(1)}, s32[2,3]{1,0:T(2,128)}, u32[]{:S(2)}) copy-start(s32[2,3]{1,0:T(2,128)} %nbr_ref.3) | copy-start | bytes 76
  18.8 23.0 %copy-start = (bf16[1,84,512]{2,1,0:T(8,128)(2,1)S(1)}, bf16[1,84,512]{2,1,0:T(8,128)(2,1)}, u32[]{:S(2)}) copy-start(bf16[1,84,512]{2,1,0:T(8,128)(2,1)} %param.13) | copy-start | bytes 258052
  25.1 11.9 %collective-permute-start.3 = (bf16[2,84,512]{2,1,0:T(8,128)(2,1)S(1)}, bf16[2,84,512]{2,1,0:T(8,128)(2,1)S(1)}, u32[]{:S(2)}, u32[]{:S(2)}) collective-permute-start(bf16[2,84,512]{2,1,0:T(8,128)(2,1)S(1)} %get-tuple-element.25.refs_1_), channel_id=1, source_target_pairs={{0,32},{32,0},{1,33},{33,1},{2,34},{34,2},{3,35},{35,3},{4,36},{36... | collective-permute-start | bytes 516104 | tf_op jit(solution)/shard_map/ppermute | solution.py:395
  32.1 9.7 %collective-permute-start.2 = (bf16[2,84,512]{2,1,0:T(8,128)(2,1)S(1)}, bf16[2,84,512]{2,1,0:T(8,128)(2,1)S(1)}, u32[]{:S(2)}, u32[]{:S(2)}) collective-permute-start(bf16[2,84,512]{2,1,0:T(8,128)(2,1)S(1)} %get-tuple-element.23.refs_0_), channel_id=1, source_target_pairs={{0,32},{32,0},{1,33},{33,1},{2,34},{34,2},{3,35},{35,3},{4,36},{36... | collective-permute-start | bytes 516104 | tf_op jit(solution)/shard_map/ppermute | solution.py:395
  87.1 14.4 %all-to-all-start.3 = ((f32[32,16,128]{2,1,0:T(8,128)}), f32[32,16,128]{2,1,0:T(8,128)S(1)}, u32[]{:S(2)}, u32[]{:S(2)}) async-start(f32[32,16,128]{2,1,0:T(8,128)} %get-tuple-element.32), calls=%async_computation.3 | async-start | bytes 524288 | tf_op jit(solution)/shard_map/all_to_all | solution.py:314
where the time goes:
time: 103 us; the launch traced here: 102 us
  blocking collectives  42.6 us (41%)
  Pallas kernels  20 us (19%)
  starting transfers between devices  18.6 us (18%)
  waiting for transfers between devices  17.3 us (17%)
  local copies, waits for them, and re-layouts  3.04 us (3%)
    all_to_all x3, blocking collectives, exchange(): return lax.all_to_all(blocks, axis, split_axis=0, concat_axis=0, tiled=True)  42.6 us
    pallas_call x9, Pallas kernels, call(): pl.pallas_call(kernel, out_shape=outs, in_specs=[SMEM if i in smem else V...  20 us
    ppermute x2, waiting for transfers between devices, step(): other.append(lax.ppermute(got[0], 'member', [(0, 1), (1, 0)]))  9.62 us
    all_to_all x1, waiting for transfers between devices, exchange(): return lax.all_to_all(blocks, axis, split_axis=0, concat_axis=0, tiled=True)  7.65 us
    ppermute x2, starting transfers between devices, step(): other.append(lax.ppermute(got[0], 'member', [(0, 1), (1, 0)]))  7.08 us
    all_to_all x1, starting transfers between devices, exchange(): return lax.all_to_all(blocks, axis, split_axis=0, concat_axis=0, tiled=True)  5.33 us
    ppermute x1, starting transfers between devices, step(): from_pair = lax.ppermute(pooled, 'space', pairs)  3.47 us
    ppermute x1, starting transfers between devices, step(): from_next = lax.ppermute(pooled, 'space', nexts)  2.76 us
  transfers between devices with their start and end apart: 5, of which 3 were waited for; matrix products, arithmetic and copies ran while one was open for 1% of the time, Pallas kernels for 3%

commit v1 on v0

--- a/solution.py
+++ b/solution.py
@@ -4,6 +4,7 @@
 import jax.numpy as jnp
 from jax import lax
 from jax.experimental import pallas as pl
+from jax.experimental.layout import Layout, with_layout_constraint
 from jax.experimental.pallas import tpu as pltpu
 from jax.sharding import PartitionSpec as P
 
@@ -15,13 +16,13 @@
 EPSILON = 1e-06
 LANES = 128
 GROUP = 4
-LOG2E = 1.4426950408889634
 
 F32 = jnp.float32
 BF16 = jnp.bfloat16
 
 VMEM = pl.BlockSpec(memory_space=pltpu.VMEM)
 SMEM = pl.BlockSpec(memory_space=pltpu.SMEM)
+HBM = pl.BlockSpec(memory_space=pl.ANY)
 NT = (((1,), (1,)), ((), ()))
 
 
@@ -33,16 +34,17 @@
     return lax.dot_general(a, b, NT, preferred_element_type=F32)
 
 
-def call(kernel, outs, args, smem=(), scratch=(), limit=24, work=0):
+def call(kernel, outs, args, smem=(), hbm=(), scratch=(), out_specs=None, limit=24, work=0):
     many = isinstance(outs, list)
     kept = [
-        a if i in smem else pltpu.with_memory_space_constraint(a, pltpu.VMEM) for i, a in enumerate(args)
+        a if i in smem or i in hbm else pltpu.with_memory_space_constraint(a, pltpu.VMEM)
+        for i, a in enumerate(args)
     ]
     return pl.pallas_call(
         kernel,
         out_shape=outs,
-        in_specs=[SMEM if i in smem else VMEM for i in range(len(args))],
-        out_specs=[VMEM] * len(outs) if many else VMEM,
+        in_specs=[SMEM if i in smem else HBM if i in hbm else VMEM for i in range(len(args))],
+        out_specs=out_specs or ([VMEM] * len(outs) if many else VMEM),
         scratch_shapes=list(scratch),
         compiler_params=pltpu.CompilerParams(vmem_limit_bytes=limit << 20),
         cost_estimate=pl.CostEstimate(flops=work, transcendentals=0, bytes_accessed=work // 100),
@@ -59,8 +61,16 @@
     return counts
 
 
-def pool_kernel(enc_ref, grid_ref, pooled_ref):
+def pool_kernel(enc_hbm, grid_hbm, pooled_ref, enc_ref, grid_ref, sems):
+    copies = [
+        pltpu.make_async_copy(enc_hbm, enc_ref, sems.at[0]),
+        pltpu.make_async_copy(grid_hbm, grid_ref, sems.at[1]),
+    ]
+    for copy in copies:
+        copy.start()
+    copies[0].wait()
     counts = counts_of(enc_ref[...], grid_ref.shape[1]).astype(BF16)
+    copies[1].wait()
     pooled_ref[...] = dot(grid_ref[...], counts) * (1.0 / K_ENC)
 
 
@@ -107,6 +117,8 @@
         inputs_ref[m * tok : (m + 1) * tok, :] = (normed * gain[m : m + 1] + shift[m : m + 1]).astype(BF16)
     for c in range(3):
         part = dot(inputs_ref[...], w_qkv_ref[:, c * d : (c + 1) * d])
+        if c == 0:
+            part = part * HD ** (-0.5)
         project_ref[:, c * d : (c + 1) * d] = part.astype(BF16)
     counts = counts_of(dec_ref[...], tok).T.astype(BF16)
     counts_ref[:, :tok] = counts
@@ -164,13 +176,13 @@
             kv_ref[m, 2 * tok :, lo : lo + d] = part[(2 * m + 1) * tok : (2 * m + 2) * tok]
     head_of = lax.broadcasted_iota(jnp.int32, (WIN, wide), 1) // HD
 
-    def attend(m, carry):
+    def attend(m):
         for w in range(wins):
             starts = [(wins + w) * WIN]
             for j in range(nbr_ref.shape[1]):
                 reach = lax.rem(nbr_ref[w, j] - first - w + 2 + windows, windows) + w
                 starts.append(pl.multiple_of(reach * WIN, WIN))
-            row = pl.multiple_of(m * tok + w * WIN, WIN)
+            row = m * tok + w * WIN
             for g in range(HEADS // GROUP):
                 lo = g * wide
                 q = project_ref[pl.ds(begin * tok + row, WIN), lo : lo + wide]
@@ -180,18 +192,18 @@
                 values = jnp.concatenate(
                     [kv_ref[m, pl.ds(s, WIN), d + lo : d + lo + wide] for s in starts], axis=0
                 )
-                scores = dot_nt(spread, keys) * (HD ** (-0.5) * LOG2E)
+                scores = dot_nt(spread, keys)
                 top = jnp.max(scores, axis=-1, keepdims=True)
-                weights = jnp.exp2(scores - top)
+                weights = jnp.exp(scores - top)
                 weights = weights * (1.0 / jnp.sum(weights, axis=-1, keepdims=True))
                 mixed = dot(weights.astype(BF16), values)
                 out = mixed[:WIN]
                 for h in range(1, GROUP):
                     out = jnp.where(head_of == h, mixed[h * WIN : (h + 1) * WIN], out)
                 att_ref[pl.ds(row, WIN), lo : lo + wide] = out.astype(BF16)
-        return carry
-
-    lax.fori_loop(0, members, attend, 0)
+
+    for m in range(members):
+        attend(m)
     mixed = dot(att_ref[...], w_o_ref[...])
     for m in range(members):
         updated = states_ref[...] + mixed[m * tok : (m + 1) * tok]
@@ -245,8 +257,8 @@
 def slope_kernel(
     members, members_all, stat_ref, target_ref, *refs
 ):
-    parts = (len(refs) - 4) // 3
-    pred_ref, grad_ref, score_ref, pack_ref = refs[-4:]
+    parts = (len(refs) - 3) // 3
+    grad_ref, score_ref, pack_ref = refs[-3:]
     xs = [r[i] for r in refs[: 2 * parts] for i in range(r.shape[0])]
     feats = [r.at[i] for r in refs[2 * parts : 3 * parts] for i in range(r.shape[0])]
     xf = [x.astype(F32) for x in xs]
@@ -273,7 +285,6 @@
         coef[j, i] = value
     acc = None
     for i in range(members):
-        pred_ref[i] = xs[i]
         slope = pull[:, i : i + 1] * (xf[i] - truth)
         for j in range(2 * members):
             if j != i:
@@ -293,15 +304,16 @@
     out_ref[...] = jnp.broadcast_to(both[None], out_ref.shape)
 
 
-def spread_kernel(scale, recv_ref, out_ref, score_ref):
+def spread_kernel(recv_ref, out_ref, score_ref):
     rows = out_ref.shape[1]
     total = jnp.sum(recv_ref[...], axis=0)
     out_ref[...] = jnp.broadcast_to(total[:rows][None], out_ref.shape)
-    score_ref[...] = total[rows:] * scale
-
-
-def final_kernel(recv_ref, out_ref, pack_ref):
+    score_ref[...] = total[rows:]
+
+
+def final_kernel(scale, recv_ref, score_ref, out_ref, objective_ref, pack_ref):
     v, d = out_ref.shape
+    objective_ref[0] = jnp.max(score_ref[...]) * scale
     pack_ref[...] = recv_ref[...].reshape(pack_ref.shape)
     grad = pack_ref[...]
     square = jnp.sum(jnp.sum(grad * grad, axis=0, keepdims=True), axis=1, keepdims=True)
@@ -337,7 +349,18 @@
     grid = grid_in[0]
     truth = target[0]
 
-    pooled = call(pool_kernel, pltpu.VMEM((v, tok), F32), (enc_index.T, grid), work=4 * 10**9)
+    pooled = call(
+        pool_kernel,
+        pltpu.VMEM((v, tok), F32),
+        (enc_index.T, grid),
+        hbm=(0, 1),
+        scratch=(
+            pltpu.VMEM((enc_index.shape[1], tok), jnp.int32),
+            pltpu.VMEM((v, points), BF16),
+            pltpu.SemaphoreType.DMA((2,)),
+        ),
+        work=4 * 10**9,
+    )
     pairs = [(i, i ^ 1) for i in range(space)]
     nexts = [(i, (i + 1 if i % 2 else i - 1) % space) for i in range(space)]
     from_pair = lax.ppermute(pooled, "space", pairs)
@@ -393,6 +416,10 @@
         own.append(got[0])
         feats.append(got[1])
         other.append(lax.ppermute(got[0], "member", [(0, 1), (1, 0)]))
+    pred = jnp.concatenate([x.transpose(1, 0, 2) for x in own], axis=1)
+    pred = with_layout_constraint(pred, Layout(major_to_minor=(0, 1, 2)))
+    pred, other[-1] = lax.optimization_barrier((pred, other[-1]))
+    pred = pred.transpose(1, 0, 2)
     members_all = members * lax.axis_size("member")
     stats = call(
         functools.partial(stats_kernel, members),
@@ -402,10 +429,9 @@
     )
     stats = exchange(stats, "space")
     rows = -(-v * d // (LANES * space * 8)) * 8
-    pred, grad, score = call(
+    grad, score = call(
         functools.partial(slope_kernel, members, members_all),
         [
-            jax.ShapeDtypeStruct((members, v, points), BF16),
             pltpu.VMEM((space, rows, LANES), BF16),
             pltpu.VMEM((8, LANES), F32),
         ],
@@ -417,19 +443,20 @@
     share = call(share_kernel, pltpu.VMEM((peers, rows + 8, LANES), F32), (grad, score))
     share = exchange(share, ("dp", "member"))
     scale = 1.0 / (lax.axis_size("dp") * (v * points * space) ** 0.5)
-    spread, objective = call(
-        functools.partial(spread_kernel, scale),
+    spread, score = call(
+        spread_kernel,
         [pltpu.VMEM((space, rows, LANES), F32), pltpu.VMEM((8, LANES), F32)],
         (share,),
     )
     spread = exchange(spread, "space")
-    unit = call(
-        final_kernel,
-        jax.ShapeDtypeStruct((v, d), F32),
-        (spread,),
+    unit, objective = call(
+        functools.partial(final_kernel, scale),
+        [jax.ShapeDtypeStruct((v, d), F32), jax.ShapeDtypeStruct((1,), F32)],
+        (spread, score),
+        out_specs=[VMEM, SMEM],
         scratch=(pltpu.VMEM((space * rows, LANES), F32),),
     )
-    return (pred[None], objective[0, 0], unit)
+    return (pred[None], objective.reshape(()), unit)
 
 
 def solution(mesh):

time: 103 us -> 100 us (0.971)
  blocking collectives: 42.6 us -> 56 us
  waiting for transfers between devices: 17.3 us -> 8.26 us
  starting transfers between devices: 18.6 us -> 13.5 us
  Pallas kernels: 20 us -> 18.1 us
  local copies, waits for them, and re-layouts: 3.04 us -> 1.89 us
  other arithmetic: 0 us -> 1.09 us
    all_to_all x3 -> x4, blocking collectives: 42.6 us -> 56 us  [exchange(): return lax.all_to_all(blocks, axis, split_axis=0, concat_axis=0, tiled=True)]
    all_to_all x1 -> x0, waiting for transfers between devices: 7.65 us -> none  [exchange(): return lax.all_to_all(blocks, axis, split_axis=0, concat_axis=0, tiled=True)]
    all_to_all x1 -> x0, starting transfers between devices: 5.33 us -> none  [exchange(): return lax.all_to_all(blocks, axis, split_axis=0, concat_axis=0, tiled=True)]
    pallas_call x9, Pallas kernels: 20 us -> 18.1 us  [call(): pl.pallas_call(kernel, out_shape=outs, in_specs=[SMEM if i in smem else H...]
    ppermute x2, waiting for transfers between devices: 9.62 us -> 8.25 us  [step(): other.append(lax.ppermute(got[0], 'member', [(0, 1), (1, 0)]))]
    concatenate x0 -> x1, other arithmetic: none -> 1.09 us  [step(): pred = jnp.concatenate([x.transpose(1, 0, 2) for x in own], axis=1)]
    unnamed x27 -> x26, local copies, waits for them, and re-layouts: 2.53 us -> 1.62 us
  transfers between devices with their start and end apart: 5 -> 4, of which waited for: 3 -> 2; matrix products, arithmetic and copies ran while one was open for 1% -> 1% of each run, Pallas kernels for 3% -> 3%
where the time goes in v1:
time: 100 us; the launch traced here: 99.8 us
  blocking collectives  56 us (56%)
  Pallas kernels  18.1 us (18%)
  starting transfers between devices  13.5 us (14%)
  waiting for transfers between devices  8.26 us (8%)
  local copies, waits for them, and re-layouts  1.89 us (2%)
  other arithmetic  1.09 us (1%)
    all_to_all x4, blocking collectives, exchange(): return lax.all_to_all(blocks, axis, split_axis=0, concat_axis=0, tiled=True)  56 us
    pallas_call x9, Pallas kernels, call(): pl.pallas_call(kernel, out_shape=outs, in_specs=[SMEM if i in smem else H...  18.1 us
    ppermute x2, waiting for transfers between devices, step(): other.append(lax.ppermute(got[0], 'member', [(0, 1), (1, 0)]))  8.25 us
    ppermute x2, starting transfers between devices, step(): other.append(lax.ppermute(got[0], 'member', [(0, 1), (1, 0)]))  7.27 us
    ppermute x1, starting transfers between devices, step(): from_pair = lax.ppermute(pooled, 'space', pairs)  3.47 us
    ppermute x1, starting transfers between devices, step(): from_next = lax.ppermute(pooled, 'space', nexts)  2.76 us
  transfers between devices with their start and end apart: 4, of which 2 were waited for; matrix products, arithmetic and copies ran while one was open for 1% of the time, Pallas kernels for 3%

profile of v1, /device:TPU:1, one launch (start us, length us, event | category | flops | bytes accessed | tf_op | source)
XLA Modules:
  0.0 99.8 jit_solution(1888311352911399786)
XLA Ops:
  0.6 0.0 copy-start.7
  0.6 0.9 copy-done.7
  1.5 0.7 copy-done.10
  2.2 0.5 shard_map.139.pooled_ref
  2.8 2.8 %collective-permute-start.1 = (f32[84,128]{1,0:T(8,128)S(1)}, f32[84,128]{1,0:T(8,128)S(1)}, u32[]{:S(2)}, u32[]{:S(2)}) collective-permute-start(f32[84,128]{1,0:T(8,128)S(1)} %shard_map.139.pooled_ref), channel_id=1, source_target_pairs={{0,31},{1,2},{2,1},{3,4},{4,3},{5,6},{6,5},{7,8},{8,7},{9,10},{10,... | collective-permute-start | bytes 129032 | tf_op jit(solution)/shard_map/ppermute | solution.py:367
  5.5 3.5 %collective-permute-start = (f32[84,128]{1,0:T(8,128)S(1)}, f32[84,128]{1,0:T(8,128)S(1)}, u32[]{:S(2)}, u32[]{:S(2)}) collective-permute-start(f32[84,128]{1,0:T(8,128)S(1)} %shard_map.139.pooled_ref), channel_id=1, source_target_pairs={{0,1},{1,0},{2,3},{3,2},{4,5},{5,4},{6,7},{7,6},{8,9},{9,8},{10,11... | collective-permute-start | bytes 129032 | tf_op jit(solution)/shard_map/ppermute | solution.py:366
  9.0 0.0 copy-done.3
  9.0 0.0 copy-start.2
  9.0 0.0 copy-start.4
  9.1 0.0 copy-start.8
  9.1 0.0 copy-start.12
  9.1 2.7 %shard_map.140 = (f32[128,768]{1,0:T(8,128)S(1)}, f32[4,768]{1,0:T(4,128)S(1)}, f32[4,768]{1,0:T(4,128)S(1)}, bf16[512,2304]{1,0:T(8,128)(2,1)S(1)}, bf16[512,256]{1,0:T(8,128)(2,1)S(1)}) custom-call(f32[84,128]{1,0:T(8,128)S(1)} %shard_map.139.pooled_ref, bf16[84,768]{1,0:T(8,128)(2,1)S(1)} %copy-done.3, f32[4,32]{1,0:T(4,128)S(1)} %bitcast.22, ...), custom_call_target="tpu_custom_call" | custom-call | flops 4000000000 | bytes 40000000 | tf_op jit(solution)/shard_map/pallas_call | solution.py:43
  11.8 0.0 collective-permute-done.1.next_ref
  11.8 0.0 collective-permute-done.pair_ref
  11.9 6.5 %shard_map.141 = (bf16[2,84,512]{2,1,0:T(8,128)(2,1)S(1)}, bf16[2,512,768]{2,1,0:T(8,128)(2,1)S(1)}, f32[256,768]{1,0:T(8,128)S(1)}) custom-call(s32[2,3]{1,0:T(2,128)S(1)} %copy-done.12, f32[84,128]{1,0:T(8,128)S(1)} %collective-permute-done.pair_ref, f32[84,128]{1,0:T(8,128)S(1)} %collective-permute-done.1.next_ref, bf16[84,768]{1,0:T(8,128)(2,1)S(1)} %copy-done.3, ...), custom_call_target="tpu_custom_call" | custom-call | flops 8000000000 | bytes 80000000 | tf_op jit(solution)/shard_map/pallas_call | solution.py:43
  18.4 0.0 copy-start
  18.4 5.5 %shard_map.142 = (bf16[2,84,512]{2,1,0:T(8,128)(2,1)S(1)}, bf16[2,512,768]{2,1,0:T(8,128)(2,1)S(1)}) custom-call(s32[2,3]{1,0:T(2,128)S(1)} %copy-done.12, f32[256,768]{1,0:T(8,128)S(1)} %get-tuple-element.27.pair_ref, f32[84,128]{1,0:T(8,128)S(1)} %collective-permute-done.1.next_ref, bf16[84,768]{1,0:T(8,128)(2,1)S(1)} %copy-done.3, ...), custom_call_target="tpu_custom_call" | custom-call | flops 8000000000 | bytes 80000000 | tf_op jit(solution)/shard_map/pallas_call | solution.py:43
  23.9 7.2 %collective-permute-start.2 = (bf16[2,84,512]{2,1,0:T(8,128)(2,1)S(1)}, bf16[2,84,512]{2,1,0:T(8,128)(2,1)S(1)}, u32[]{:S(2)}, u32[]{:S(2)}) collective-permute-start(bf16[2,84,512]{2,1,0:T(8,128)(2,1)S(1)} %get-tuple-element.28.refs_1_), channel_id=1, source_target_pairs={{0,32},{32,0},{1,33},{33,1},{2,34},{34,2},{3,35},{35,3},{4,36},{36... | collective-permute-start | bytes 516104 | tf_op jit(solution)/shard_map/ppermute | solution.py:418
  31.1 0.1 collective-permute-start.3
  31.2 0.1 copy.19
  31.3 0.1 copy.20
  31.4 1.1 %pad_maximum_fusion = bf16[84,4,512]{2,1,0:T(4,128)(2,1)} fusion(bf16[84,2,512]{2,1,0:T(2,128)(2,1)S(1)} %bitcast.23, bf16[84,2,512]{2,1,0:T(2,128)(2,1)S(1)} %bitcast.24), kind=kLoop, calls=%fused_computation | loop fusion | flops 688128 | bytes 688128 | tf_op jit(solution)/shard_map/concatenate | solution.py:419
  32.5 3.4 %collective-permute-done.2.refs_3_ = bf16[2,84,512]{2,1,0:T(8,128)(2,1)S(1)} collective-permute-done((bf16[2,84,512]{2,1,0:T(8,128)(2,1)S(1)}, bf16[2,84,512]{2,1,0:T(8,128)(2,1)S(1)}, u32[]{:S(2)}, u32[]{:S(2)}) %collective-permute-start.2) | collective-permute-done | bytes 172064 | tf_op jit(solution)/shard_map/ppermute | solution.py:418
  36.0 4.8 %collective-permute-done.3.refs_2_ = bf16[2,84,512]{2,1,0:T(8,128)(2,1)S(1)} collective-permute-done((bf16[2,84,512]{2,1,0:T(8,128)(2,1)S(1)}, bf16[2,84,512]{2,1,0:T(8,128)(2,1)S(1)}, u32[]{:S(2)}, u32[]{:S(2)}) %collective-permute-start.3) | collective-permute-done | bytes 172064 | tf_op jit(solution)/shard_map/ppermute | solution.py:418
  40.8 0.0 copy-done
  40.8 0.8 shard_map.143
  41.6 16.8 %all_to_all.20.stat_ref = f32[32,1,128]{2,1,0:T(1,128)S(1)} all-to-all(f32[32,1,128]{2,1,0:T(1,128)S(1)} %shard_map.143), channel_id=1, replica_groups=mesh['dp'=4,'member'=2,'space'=32] {'space'}, dimensions={0} | all-to-all | bytes 32768 | tf_op jit(solution)/shard_map/all_to_all | solution.py:326
  58.3 1.1 %shard_map.144 = (bf16[32,16,128]{2,1,0:T(8,128)(2,1)S(1)}, f32[8,128]{1,0:T(8,128)S(1)}) custom-call(f32[32,1,128]{2,1,0:T(1,128)S(1)} %all_to_all.20.stat_ref, bf16[84,512]{1,0:T(8,128)(2,1)S(1)} %bitcast.16, bf16[2,84,512]{2,1,0:T(8,128)(2,1)S(1)} %get-tuple-element.26.refs_0_, bf16[2,84,512]{2,1,0:T(8,128)(2,1)S(1)} %get-tuple-element.28.refs_1_, ...), custom_call_target="tpu_custom_call" | custom-call | tf_op jit(solution)/shard_map/pallas_call | solution.py:43
  59.4 11.4 %all_to_all.21.recv_ref = bf16[32,16,128]{2,1,0:T(8,128)(2,1)S(1)} all-to-all(bf16[32,16,128]{2,1,0:T(8,128)(2,1)S(1)} %get-tuple-element.33), channel_id=1, replica_groups=mesh['dp'=4,'member'=2,'space'=32] {'space'}, dimensions={0} | all-to-all | bytes 262144 | tf_op jit(solution)/shard_map/all_to_all | solution.py:326
  70.9 13.9 %all_to_all.22.recv_ref = f32[8,24,128]{2,1,0:T(8,128)S(1)} all-to-all(f32[8,24,128]{2,1,0:T(8,128)S(1)} %shard_map.145), channel_id=1, replica_groups=mesh['dp'=4,'member'=2,'space'=32] {'dp','member'}, dimensions={0} | all-to-all | bytes 196608 | tf_op jit(solution)/shard_map/all_to_all | solution.py:326
  84.8 13.9 %all_to_all.23.recv_ref = f32[32,16,128]{2,1,0:T(8,128)S(1)} all-to-all(f32[32,16,128]{2,1,0:T(8,128)S(1)} %get-tuple-element.35), channel_id=1, replica_groups=mesh['dp'=4,'member'=2,'space'=32] {'space'}, dimensions={0} | all-to-all | bytes 524288 | tf_op jit(solution)/shard_map/all_to_all | solution.py:326
  98.8 0.9 shard_map.147
  (18 shorter events, 0.1 us)
Async XLA Ops:
  0.6 0.9 copy-start.7
  1.5 0.7 copy-start.10
  2.2 6.8 %copy-start.1 = (bf16[768,2304]{1,0:T(8,128)(2,1)S(1)}, bf16[768,2304]{1,0:T(8,128)(2,1)}, u32[]{:S(2)}) copy-start(bf16[768,2304]{1,0:T(8,128)(2,1)} %w_qkv_ref.5) | copy-start | bytes 10616836
  2.2 6.8 %copy-start.3 = (bf16[84,768]{1,0:T(8,128)(2,1)S(1)}, bf16[84,768]{1,0:T(8,128)(2,1)}, u32[]{:S(2)}) copy-start(bf16[84,768]{1,0:T(8,128)(2,1)} %w_in_ref.5) | copy-start | bytes 387076
  2.2 6.8 %copy-start.5 = (f32[32,768]{1,0:T(8,128)S(1)}, f32[32,768]{1,0:T(8,128)}, u32[]{:S(2)}) copy-start(f32[32,768]{1,0:T(8,128)} %w_gamma_ref.1) | copy-start | bytes 294916
  2.2 6.8 %copy-start.6 = (f32[32,768]{1,0:T(8,128)S(1)}, f32[32,768]{1,0:T(8,128)}, u32[]{:S(2)}) copy-start(f32[32,768]{1,0:T(8,128)} %w_beta_ref.1) | copy-start | bytes 294916
  2.2 6.8 %copy-start.9 = (s32[512,3]{0,1:T(4,128)S(1)}, s32[512,3]{0,1:T(4,128)}, u32[]{:S(2)}) copy-start(s32[512,3]{0,1:T(4,128)} %param.17) | copy-start | bytes 18436
  2.2 6.8 %copy-start.11 = (f32[1,4,32]{2,1,0:T(4,128)S(1)}, f32[1,4,32]{2,1,0:T(4,128)}, u32[]{:S(2)}) copy-start(f32[1,4,32]{2,1,0:T(4,128)} %param.14) | copy-start | bytes 1540
  2.8 9.0 %collective-permute-start.1 = (f32[84,128]{1,0:T(8,128)S(1)}, f32[84,128]{1,0:T(8,128)S(1)}, u32[]{:S(2)}, u32[]{:S(2)}) collective-permute-start(f32[84,128]{1,0:T(8,128)S(1)} %shard_map.139.pooled_ref), channel_id=1, source_target_pairs={{0,31},{1,2},{2,1},{3,4},{4,3},{5,6},{6,5},{7,8},{8,7},{9,10},{10,... | collective-permute-start | bytes 129032 | tf_op jit(solution)/shard_map/ppermute | solution.py:367
  5.5 6.3 %collective-permute-start = (f32[84,128]{1,0:T(8,128)S(1)}, f32[84,128]{1,0:T(8,128)S(1)}, u32[]{:S(2)}, u32[]{:S(2)}) collective-permute-start(f32[84,128]{1,0:T(8,128)S(1)} %shard_map.139.pooled_ref), channel_id=1, source_target_pairs={{0,1},{1,0},{2,3},{3,2},{4,5},{5,4},{6,7},{7,6},{8,9},{9,8},{10,11... | collective-permute-start | bytes 129032 | tf_op jit(solution)/shard_map/ppermute | solution.py:366
  9.0 2.8 %copy-start.2 = (bf16[768,768]{1,0:T(8,128)(2,1)S(1)}, bf16[768,768]{1,0:T(8,128)(2,1)}, u32[]{:S(2)}) copy-start(bf16[768,768]{1,0:T(8,128)(2,1)} %w_o_ref.3) | copy-start | bytes 3538948
  9.0 2.8 %copy-start.4 = (bf16[84,768]{1,0:T(8,128)(2,1)S(1)}, bf16[84,768]{1,0:T(8,128)(2,1)}, u32[]{:S(2)}) copy-start(bf16[84,768]{1,0:T(8,128)(2,1)} %readout_ref.3) | copy-start | bytes 387076
  9.1 2.8 %copy-start.8 = (bf16[1,84,512]{2,1,0:T(8,128)(2,1)S(1)}, bf16[1,84,512]{2,1,0:T(8,128)(2,1)}, u32[]{:S(2)}) copy-start(bf16[1,84,512]{2,1,0:T(8,128)(2,1)} %param.12) | copy-start | bytes 258052
  9.1 2.8 %copy-start.12 = (s32[2,3]{1,0:T(2,128)S(1)}, s32[2,3]{1,0:T(2,128)}, u32[]{:S(2)}) copy-start(s32[2,3]{1,0:T(2,128)} %nbr_ref.3) | copy-start | bytes 76
  18.4 22.4 %copy-start = (bf16[1,84,512]{2,1,0:T(8,128)(2,1)S(1)}, bf16[1,84,512]{2,1,0:T(8,128)(2,1)}, u32[]{:S(2)}) copy-start(bf16[1,84,512]{2,1,0:T(8,128)(2,1)} %param.13) | copy-start | bytes 258052
  23.9 12.1 %collective-permute-start.2 = (bf16[2,84,512]{2,1,0:T(8,128)(2,1)S(1)}, bf16[2,84,512]{2,1,0:T(8,128)(2,1)S(1)}, u32[]{:S(2)}, u32[]{:S(2)}) collective-permute-start(bf16[2,84,512]{2,1,0:T(8,128)(2,1)S(1)} %get-tuple-element.28.refs_1_), channel_id=1, source_target_pairs={{0,32},{32,0},{1,33},{33,1},{2,34},{34,2},{3,35},{35,3},{4,36},{36... | collective-permute-start | bytes 516104 | tf_op jit(solution)/shard_map/ppermute | solution.py:418
  31.1 9.7 %collective-permute-start.3 = (bf16[2,84,512]{2,1,0:T(8,128)(2,1)S(1)}, bf16[2,84,512]{2,1,0:T(8,128)(2,1)S(1)}, u32[]{:S(2)}, u32[]{:S(2)}) collective-permute-start(bf16[2,84,512]{2,1,0:T(8,128)(2,1)S(1)} %get-tuple-element.26.refs_0_), channel_id=1, source_target_pairs={{0,32},{32,0},{1,33},{33,1},{2,34},{34,2},{3,35},{35,3},{4,36},{36... | collective-permute-start | bytes 516104 | tf_op jit(solution)/shard_map/ppermute | solution.py:418

commit v2 on v1

--- a/solution.py
+++ b/solution.py
@@ -16,13 +16,14 @@
 EPSILON = 1e-06
 LANES = 128
 GROUP = 4
+CHUNKS = (2, 1, 1)
 
 F32 = jnp.float32
 BF16 = jnp.bfloat16
 
 VMEM = pl.BlockSpec(memory_space=pltpu.VMEM)
 SMEM = pl.BlockSpec(memory_space=pltpu.SMEM)
-HBM = pl.BlockSpec(memory_space=pl.ANY)
+HBM = pl.BlockSpec(memory_space=pltpu.HBM)
 NT = (((1,), (1,)), ((), ()))
 
 
@@ -37,7 +38,7 @@
 def call(kernel, outs, args, smem=(), hbm=(), scratch=(), out_specs=None, limit=24, work=0):
     many = isinstance(outs, list)
     kept = [
-        a if i in smem or i in hbm else pltpu.with_memory_space_constraint(a, pltpu.VMEM)
+        a if i in smem else pltpu.with_memory_space_constraint(a, pltpu.HBM if i in hbm else pltpu.VMEM)
         for i, a in enumerate(args)
     ]
     return pl.pallas_call(
@@ -298,28 +299,36 @@
     grad_ref[...] = pack_ref[...].astype(BF16).reshape(grad_ref.shape)
 
 
-def share_kernel(recv_ref, score_ref, out_ref):
+def share_kernel(spare, recv_ref, score_ref, out_ref):
     total = jnp.sum(recv_ref[...].astype(F32), axis=0)
-    both = jnp.concatenate([total, score_ref[...]], axis=0)
-    out_ref[...] = jnp.broadcast_to(both[None], out_ref.shape)
-
-
-def spread_kernel(recv_ref, out_ref, score_ref):
-    rows = out_ref.shape[1]
+    rows = lax.broadcasted_iota(jnp.int32, total.shape, 0)
+    last = lax.axis_index("space") == lax.axis_size("space") - 1
+    score = jnp.broadcast_to(score_ref[0:1, :], total.shape)
+    total = jnp.where(jnp.logical_and(last, rows >= spare), score, total)
+    out_ref[...] = jnp.broadcast_to(total[None], out_ref.shape)
+
+
+def spread_kernel(spare, recv_ref, out_ref):
     total = jnp.sum(recv_ref[...], axis=0)
-    out_ref[...] = jnp.broadcast_to(total[:rows][None], out_ref.shape)
-    score_ref[...] = total[rows:]
-
-
-def final_kernel(scale, recv_ref, score_ref, out_ref, objective_ref, pack_ref):
+    rows = lax.broadcasted_iota(jnp.int32, total.shape, 0)
+    last = lax.axis_index("space") == lax.axis_size("space") - 1
+    high = total.astype(BF16)
+    low = (total - high.astype(F32)).astype(BF16)
+    sent = jnp.where(jnp.logical_and(last, rows > spare), low.astype(F32), high.astype(F32)).astype(BF16)
+    out_ref[...] = jnp.broadcast_to(sent[None], out_ref.shape)
+
+
+def final_kernel(scale, recv_ref, out_ref, objective_ref, pack_ref):
     v, d = out_ref.shape
-    objective_ref[0] = jnp.max(score_ref[...]) * scale
-    pack_ref[...] = recv_ref[...].reshape(pack_ref.shape)
-    grad = pack_ref[...]
+    used = v * d // LANES
+    pack_ref[...] = recv_ref[...].reshape(pack_ref.shape).astype(F32)
+    tail = pack_ref[used : used + 8, :]
+    objective_ref[0] = jnp.max(tail[0:1, :] + tail[1:2, :]) * scale
+    grad = pack_ref[:used, :]
     square = jnp.sum(jnp.sum(grad * grad, axis=0, keepdims=True), axis=1, keepdims=True)
-    scale = 1.0 / jnp.sqrt(square / (v * d) + EPSILON)
+    factor = 1.0 / jnp.sqrt(square / (v * d) + EPSILON)
     for c in range(d // LANES):
-        out_ref[:, c * LANES : (c + 1) * LANES] = pack_ref[c * v : (c + 1) * v, :] * scale
+        out_ref[:, c * LANES : (c + 1) * LANES] = pack_ref[c * v : (c + 1) * v, :] * factor
 
 
 def exchange(blocks, axis):
@@ -380,8 +389,8 @@
     )
     own, other, feats = [], [], []
     halo = (from_pair, from_next)
-    some = members // 2
-    for begin in range(0, members, some):
+    begin = 0
+    for some in CHUNKS:
         outs = [pltpu.VMEM((some, v, points), BF16), pltpu.VMEM((some, points, d), BF16)]
         if begin == 0:
             outs.append(pltpu.VMEM((2 * tok, d), F32))
@@ -416,6 +425,7 @@
         own.append(got[0])
         feats.append(got[1])
         other.append(lax.ppermute(got[0], "member", [(0, 1), (1, 0)]))
+        begin += some
     pred = jnp.concatenate([x.transpose(1, 0, 2) for x in own], axis=1)
     pred = with_layout_constraint(pred, Layout(major_to_minor=(0, 1, 2)))
     pred, other[-1] = lax.optimization_barrier((pred, other[-1]))
@@ -440,19 +450,21 @@
     )
     grad = exchange(grad, "space")
     peers = lax.axis_size("dp") * lax.axis_size("member")
-    share = call(share_kernel, pltpu.VMEM((peers, rows + 8, LANES), F32), (grad, score))
+    spare = v * d // LANES - (space - 1) * rows
+    assert 0 < spare <= rows - 2
+    share = call(
+        functools.partial(share_kernel, spare), pltpu.VMEM((peers, rows, LANES), F32), (grad, score)
+    )
     share = exchange(share, ("dp", "member"))
     scale = 1.0 / (lax.axis_size("dp") * (v * points * space) ** 0.5)
-    spread, score = call(
-        spread_kernel,
-        [pltpu.VMEM((space, rows, LANES), F32), pltpu.VMEM((8, LANES), F32)],
-        (share,),
+    spread = call(
+        functools.partial(spread_kernel, spare), pltpu.VMEM((space, rows, LANES), BF16), (share,)
     )
     spread = exchange(spread, "space")
     unit, objective = call(
         functools.partial(final_kernel, scale),
         [jax.ShapeDtypeStruct((v, d), F32), jax.ShapeDtypeStruct((1,), F32)],
-        (spread, score),
+        (spread,),
         out_specs=[VMEM, SMEM],
         scratch=(pltpu.VMEM((space * rows, LANES), F32),),
     )

time: 100 us -> 93.2 us (0.932)
  blocking collectives: 56 us -> 44.9 us
  starting transfers between devices: 13.5 us -> 19 us
  waiting for transfers between devices: 8.26 us -> 6.73 us
  Pallas kernels: 18.1 us -> 19.6 us
  local copies, waits for them, and re-layouts: 1.89 us -> 0.46 us
    all_to_all x4, blocking collectives: 56 us -> 44.9 us  [exchange(): return lax.all_to_all(blocks, axis, split_axis=0, concat_axis=0, tiled=True)]
    ppermute x2 -> x3, starting transfers between devices: 7.27 us -> 12.7 us  [step(): other.append(lax.ppermute(got[0], 'member', [(0, 1), (1, 0)]))]
    unnamed x26 -> x22, local copies, waits for them, and re-layouts: 1.62 us -> 0.06 us
    pallas_call x9 -> x10, Pallas kernels: 18.1 us -> 19.6 us  [call(): pl.pallas_call(kernel, out_shape=outs, in_specs=[SMEM if i in smem else H...]
    ppermute x2 -> x3, waiting for transfers between devices: 8.25 us -> 6.73 us  [step(): other.append(lax.ppermute(got[0], 'member', [(0, 1), (1, 0)]))]
  transfers between devices with their start and end apart: 4 -> 5, of which waited for: 2 -> 1; matrix products, arithmetic and copies ran while one was open for 1% -> 2% of each run, Pallas kernels for 3% -> 10%
where the time goes in v2:
time: 93.2 us; the launch traced here: 93 us
  blocking collectives  44.9 us (48%)
  Pallas kernels  19.6 us (21%)
  starting transfers between devices  19 us (20%)
  waiting for transfers between devices  6.73 us (7%)
  other arithmetic  1.31 us (1%)
  between operations  1.02 us (1%)
    all_to_all x4, blocking collectives, exchange(): return lax.all_to_all(blocks, axis, split_axis=0, concat_axis=0, tiled=True)  44.9 us
    pallas_call x10, Pallas kernels, call(): pl.pallas_call(kernel, out_shape=outs, in_specs=[SMEM if i in smem else H...  19.6 us
    ppermute x3, starting transfers between devices, step(): other.append(lax.ppermute(got[0], 'member', [(0, 1), (1, 0)]))  12.7 us
    ppermute x3, waiting for transfers between devices, step(): other.append(lax.ppermute(got[0], 'member', [(0, 1), (1, 0)]))  6.73 us
    ppermute x1, starting transfers between devices, step(): from_pair = lax.ppermute(pooled, 'space', pairs)  3.46 us
    ppermute x1, starting transfers between devices, step(): from_next = lax.ppermute(pooled, 'space', nexts)  2.76 us
  transfers between devices with their start and end apart: 5, of which 1 were waited for; matrix products, arithmetic and copies ran while one was open for 2% of the time, Pallas kernels for 10%

profile of v2, /device:TPU:1, one launch (start us, length us, event | category | flops | bytes accessed | tf_op | source)
XLA Modules:
  0.0 93.0 jit_solution(10963119432967380313)
XLA Ops:
  0.7 1.2 %shard_map.139.pooled_ref = f32[84,128]{1,0:T(8,128)S(1)} custom-call(s32[4,128]{1,0:T(4,128)} %bitcast.26, bf16[84,512]{1,0:T(8,128)(2,1)} %bitcast.18), custom_call_target="tpu_custom_call" | custom-call | flops 4000000000 | bytes 40000000 | tf_op jit(solution)/shard_map/pallas_call | solution.py:44
  1.9 2.8 %collective-permute-start.1 = (f32[84,128]{1,0:T(8,128)S(1)}, f32[84,128]{1,0:T(8,128)S(1)}, u32[]{:S(2)}, u32[]{:S(2)}) collective-permute-start(f32[84,128]{1,0:T(8,128)S(1)} %shard_map.139.pooled_ref), channel_id=1, source_target_pairs={{0,31},{1,2},{2,1},{3,4},{4,3},{5,6},{6,5},{7,8},{8,7},{9,10},{10,... | collective-permute-start | bytes 129032 | tf_op jit(solution)/shard_map/ppermute | solution.py:376
  4.7 3.5 %collective-permute-start = (f32[84,128]{1,0:T(8,128)S(1)}, f32[84,128]{1,0:T(8,128)S(1)}, u32[]{:S(2)}, u32[]{:S(2)}) collective-permute-start(f32[84,128]{1,0:T(8,128)S(1)} %shard_map.139.pooled_ref), channel_id=1, source_target_pairs={{0,1},{1,0},{2,3},{3,2},{4,5},{5,4},{6,7},{7,6},{8,9},{9,8},{10,11... | collective-permute-start | bytes 129032 | tf_op jit(solution)/shard_map/ppermute | solution.py:375
  8.2 0.0 copy-done.3
  8.2 0.0 copy-start.2
  8.2 0.0 copy-start.4
  8.2 0.0 copy-start.7
  8.2 0.0 copy-start.10
  8.2 2.7 %shard_map.140 = (f32[128,768]{1,0:T(8,128)S(1)}, f32[4,768]{1,0:T(4,128)S(1)}, f32[4,768]{1,0:T(4,128)S(1)}, bf16[512,2304]{1,0:T(8,128)(2,1)S(1)}, bf16[512,256]{1,0:T(8,128)(2,1)S(1)}) custom-call(f32[84,128]{1,0:T(8,128)S(1)} %shard_map.139.pooled_ref, bf16[84,768]{1,0:T(8,128)(2,1)S(1)} %copy-done.3, f32[4,32]{1,0:T(4,128)S(1)} %bitcast.23, ...), custom_call_target="tpu_custom_call" | custom-call | flops 4000000000 | bytes 40000000 | tf_op jit(solution)/shard_map/pallas_call | solution.py:44
  11.0 0.0 collective-permute-done.1.next_ref
  11.0 0.0 collective-permute-done.pair_ref
  11.0 6.5 %shard_map.141 = (bf16[2,84,512]{2,1,0:T(8,128)(2,1)S(1)}, bf16[2,512,768]{2,1,0:T(8,128)(2,1)S(1)}, f32[256,768]{1,0:T(8,128)S(1)}) custom-call(s32[2,3]{1,0:T(2,128)S(1)} %copy-done.10, f32[84,128]{1,0:T(8,128)S(1)} %collective-permute-done.pair_ref, f32[84,128]{1,0:T(8,128)S(1)} %collective-permute-done.1.next_ref, bf16[84,768]{1,0:T(8,128)(2,1)S(1)} %copy-done.3, ...), custom_call_target="tpu_custom_call" | custom-call | flops 8000000000 | bytes 80000000 | tf_op jit(solution)/shard_map/pallas_call | solution.py:44
  17.5 0.1 copy.20
  17.7 7.0 %collective-permute-start.3 = (bf16[2,84,512]{2,1,0:T(8,128)(2,1)S(1)}, bf16[2,84,512]{2,1,0:T(8,128)(2,1)S(1)}, u32[]{:S(2)}, u32[]{:S(2)}) collective-permute-start(bf16[2,84,512]{2,1,0:T(8,128)(2,1)S(1)} %get-tuple-element.26.refs_0_), channel_id=1, source_target_pairs={{0,32},{32,0},{1,33},{33,1},{2,34},{34,2},{3,35},{35,3},{4,36},{36... | collective-permute-start | bytes 516104 | tf_op jit(solution)/shard_map/ppermute | solution.py:427
  24.7 3.2 %shard_map.142 = (bf16[1,84,512]{2,1,0:T(8,128)(2,1)S(1)}, bf16[1,512,768]{2,1,0:T(8,128)(2,1)S(1)}) custom-call(s32[2,3]{1,0:T(2,128)S(1)} %copy-done.10, f32[256,768]{1,0:T(8,128)S(1)} %get-tuple-element.27.pair_ref, f32[84,128]{1,0:T(8,128)S(1)} %collective-permute-done.1.next_ref, bf16[84,768]{1,0:T(8,128)(2,1)S(1)} %copy-done.3, ...), custom_call_target="tpu_custom_call" | custom-call | flops 8000000000 | bytes 80000000 | tf_op jit(solution)/shard_map/pallas_call | solution.py:44
  27.9 0.0 copy-start
  27.9 0.3 collective-permute-start.4
  28.2 3.2 %shard_map.143 = (bf16[1,84,512]{2,1,0:T(8,128)(2,1)S(1)}, bf16[1,512,768]{2,1,0:T(8,128)(2,1)S(1)}) custom-call(s32[2,3]{1,0:T(2,128)S(1)} %copy-done.10, f32[256,768]{1,0:T(8,128)S(1)} %get-tuple-element.27.pair_ref, f32[84,128]{1,0:T(8,128)S(1)} %collective-permute-done.1.next_ref, bf16[84,768]{1,0:T(8,128)(2,1)S(1)} %copy-done.3, ...), custom_call_target="tpu_custom_call" | custom-call | flops 8000000000 | bytes 80000000 | tf_op jit(solution)/shard_map/pallas_call | solution.py:44
  31.4 0.1 copy.17
  31.5 5.4 %collective-permute-start.2 = (bf16[1,84,512]{2,1,0:T(8,128)(2,1)S(1)}, bf16[1,84,512]{2,1,0:T(8,128)(2,1)S(1)}, u32[]{:S(2)}, u32[]{:S(2)}) collective-permute-start(bf16[1,84,512]{2,1,0:T(8,128)(2,1)S(1)} %get-tuple-element.29.refs_2_), channel_id=1, source_target_pairs={{0,32},{32,0},{1,33},{33,1},{2,34},{34,2},{3,35},{35,3},{4,36},{36... | collective-permute-start | bytes 258056 | tf_op jit(solution)/shard_map/ppermute | solution.py:427
  37.0 0.1 copy.18
  37.1 1.3 %pad_maximum_fusion = bf16[84,4,512]{2,1,0:T(4,128)(2,1)} fusion(bf16[84,1,512]{2,1,0:T(2,128)(2,1)S(1)} %copy.18, bf16[84,1,512]{2,1,0:T(2,128)(2,1)S(1)} %copy.17, bf16[84,2,512]{2,1,0:T(2,128)(2,1)S(1)} %bitcast.24), kind=kLoop, calls=%fused_computation | loop fusion | flops 1032192 | bytes 688128 | tf_op jit(solution)/shard_map/concatenate | solution.py:429
  38.4 6.7 %collective-permute-done.2.refs_5_ = bf16[1,84,512]{2,1,0:T(8,128)(2,1)S(1)} collective-permute-done((bf16[1,84,512]{2,1,0:T(8,128)(2,1)S(1)}, bf16[1,84,512]{2,1,0:T(8,128)(2,1)S(1)}, u32[]{:S(2)}, u32[]{:S(2)}) %collective-permute-start.2) | collective-permute-done | bytes 86048 | tf_op jit(solution)/shard_map/ppermute | solution.py:427
  45.1 0.0 collective-permute-done.4.refs_4_
  45.1 0.0 collective-permute-done.3.refs_3_
  45.2 0.8 shard_map.144
  45.9 10.7 %all_to_all.20.stat_ref = f32[32,1,128]{2,1,0:T(1,128)S(1)} all-to-all(f32[32,1,128]{2,1,0:T(1,128)S(1)} %shard_map.144), channel_id=1, replica_groups=mesh['dp'=4,'member'=2,'space'=32] {'space'}, dimensions={0} | all-to-all | bytes 32768 | tf_op jit(solution)/shard_map/all_to_all | solution.py:335
  56.7 1.0 %shard_map.145 = (bf16[32,16,128]{2,1,0:T(8,128)(2,1)S(1)}, f32[8,128]{1,0:T(8,128)S(1)}) custom-call(f32[32,1,128]{2,1,0:T(1,128)S(1)} %all_to_all.20.stat_ref, bf16[84,512]{1,0:T(8,128)(2,1)S(1)} %bitcast.17, bf16[2,84,512]{2,1,0:T(8,128)(2,1)S(1)} %get-tuple-element.26.refs_0_, bf16[1,84,512]{2,1,0:T(8,128)(2,1)S(1)} %get-tuple-element.28.refs_1_, ...), custom_call_target="tpu_custom_call" | custom-call | tf_op jit(solution)/shard_map/pallas_call | solution.py:44
  57.7 11.4 %all_to_all.21.recv_ref = bf16[32,16,128]{2,1,0:T(8,128)(2,1)S(1)} all-to-all(bf16[32,16,128]{2,1,0:T(8,128)(2,1)S(1)} %get-tuple-element.35), channel_id=1, replica_groups=mesh['dp'=4,'member'=2,'space'=32] {'space'}, dimensions={0} | all-to-all | bytes 262144 | tf_op jit(solution)/shard_map/all_to_all | solution.py:335
  69.2 10.0 %all_to_all.22.recv_ref = f32[8,16,128]{2,1,0:T(8,128)S(1)} all-to-all(f32[8,16,128]{2,1,0:T(8,128)S(1)} %shard_map.146), channel_id=1, replica_groups=mesh['dp'=4,'member'=2,'space'=32] {'dp','member'}, dimensions={0} | all-to-all | bytes 131072 | tf_op jit(solution)/shard_map/all_to_all | solution.py:335
  79.2 12.7 %all_to_all.23.recv_ref = bf16[32,16,128]{2,1,0:T(8,128)(2,1)S(1)} all-to-all(bf16[32,16,128]{2,1,0:T(8,128)(2,1)S(1)} %shard_map.147), channel_id=1, replica_groups=mesh['dp'=4,'member'=2,'space'=32] {'space'}, dimensions={0} | all-to-all | bytes 262144 | tf_op jit(solution)/shard_map/all_to_all | solution.py:335
  91.9 0.9 shard_map.148
  (18 shorter events, 0.1 us)
Async XLA Ops:
  0.6 7.5 %copy-start.1 = (bf16[768,2304]{1,0:T(8,128)(2,1)S(1)}, bf16[768,2304]{1,0:T(8,128)(2,1)}, u32[]{:S(2)}) copy-start(bf16[768,2304]{1,0:T(8,128)(2,1)} %w_qkv_ref.7) | copy-start | bytes 10616836
  0.6 7.5 %copy-start.3 = (bf16[84,768]{1,0:T(8,128)(2,1)S(1)}, bf16[84,768]{1,0:T(8,128)(2,1)}, u32[]{:S(2)}) copy-start(bf16[84,768]{1,0:T(8,128)(2,1)} %w_in_ref.7) | copy-start | bytes 387076
  0.7 7.5 %copy-start.5 = (f32[32,768]{1,0:T(8,128)S(1)}, f32[32,768]{1,0:T(8,128)}, u32[]{:S(2)}) copy-start(f32[32,768]{1,0:T(8,128)} %w_gamma_ref.1) | copy-start | bytes 294916
  0.7 7.5 %copy-start.6 = (f32[32,768]{1,0:T(8,128)S(1)}, f32[32,768]{1,0:T(8,128)}, u32[]{:S(2)}) copy-start(f32[32,768]{1,0:T(8,128)} %w_beta_ref.1) | copy-start | bytes 294916
  0.7 7.5 %copy-start.8 = (s32[512,3]{0,1:T(4,128)S(1)}, s32[512,3]{0,1:T(4,128)}, u32[]{:S(2)}) copy-start(s32[512,3]{0,1:T(4,128)} %param.17) | copy-start | bytes 18436
  0.7 7.5 %copy-start.9 = (f32[1,4,32]{2,1,0:T(4,128)S(1)}, f32[1,4,32]{2,1,0:T(4,128)}, u32[]{:S(2)}) copy-start(f32[1,4,32]{2,1,0:T(4,128)} %param.14) | copy-start | bytes 1540
  1.9 9.0 %collective-permute-start.1 = (f32[84,128]{1,0:T(8,128)S(1)}, f32[84,128]{1,0:T(8,128)S(1)}, u32[]{:S(2)}, u32[]{:S(2)}) collective-permute-start(f32[84,128]{1,0:T(8,128)S(1)} %shard_map.139.pooled_ref), channel_id=1, source_target_pairs={{0,31},{1,2},{2,1},{3,4},{4,3},{5,6},{6,5},{7,8},{8,7},{9,10},{10,... | collective-permute-start | bytes 129032 | tf_op jit(solution)/shard_map/ppermute | solution.py:376
  4.7 6.3 %collective-permute-start = (f32[84,128]{1,0:T(8,128)S(1)}, f32[84,128]{1,0:T(8,128)S(1)}, u32[]{:S(2)}, u32[]{:S(2)}) collective-permute-start(f32[84,128]{1,0:T(8,128)S(1)} %shard_map.139.pooled_ref), channel_id=1, source_target_pairs={{0,1},{1,0},{2,3},{3,2},{4,5},{5,4},{6,7},{7,6},{8,9},{9,8},{10,11... | collective-permute-start | bytes 129032 | tf_op jit(solution)/shard_map/ppermute | solution.py:375
  8.2 2.8 %copy-start.2 = (bf16[768,768]{1,0:T(8,128)(2,1)S(1)}, bf16[768,768]{1,0:T(8,128)(2,1)}, u32[]{:S(2)}) copy-start(bf16[768,768]{1,0:T(8,128)(2,1)} %w_o_ref.5) | copy-start | bytes 3538948
  8.2 2.8 %copy-start.4 = (bf16[84,768]{1,0:T(8,128)(2,1)S(1)}, bf16[84,768]{1,0:T(8,128)(2,1)}, u32[]{:S(2)}) copy-start(bf16[84,768]{1,0:T(8,128)(2,1)} %readout_ref.5) | copy-start | bytes 387076
  8.2 2.8 %copy-start.7 = (bf16[1,84,512]{2,1,0:T(8,128)(2,1)S(1)}, bf16[1,84,512]{2,1,0:T(8,128)(2,1)}, u32[]{:S(2)}) copy-start(bf16[1,84,512]{2,1,0:T(8,128)(2,1)} %param.12) | copy-start | bytes 258052
  8.2 2.8 %copy-start.10 = (s32[2,3]{1,0:T(2,128)S(1)}, s32[2,3]{1,0:T(2,128)}, u32[]{:S(2)}) copy-start(s32[2,3]{1,0:T(2,128)} %nbr_ref.5) | copy-start | bytes 76
  17.7 27.5 %collective-permute-start.3 = (bf16[2,84,512]{2,1,0:T(8,128)(2,1)S(1)}, bf16[2,84,512]{2,1,0:T(8,128)(2,1)S(1)}, u32[]{:S(2)}, u32[]{:S(2)}) collective-permute-start(bf16[2,84,512]{2,1,0:T(8,128)(2,1)S(1)} %get-tuple-element.26.refs_0_), channel_id=1, source_target_pairs={{0,32},{32,0},{1,33},{33,1},{2,34},{34,2},{3,35},{35,3},{4,36},{36... | collective-permute-start | bytes 516104 | tf_op jit(solution)/shard_map/ppermute | solution.py:427
  27.9 17.3 %copy-start = (bf16[1,84,512]{2,1,0:T(8,128)(2,1)S(1)}, bf16[1,84,512]{2,1,0:T(8,128)(2,1)}, u32[]{:S(2)}) copy-start(bf16[1,84,512]{2,1,0:T(8,128)(2,1)} %param.13) | copy-start | bytes 258052
  27.9 17.2 %collective-permute-start.4 = (bf16[1,84,512]{2,1,0:T(8,128)(2,1)S(1)}, bf16[1,84,512]{2,1,0:T(8,128)(2,1)S(1)}, u32[]{:S(2)}, u32[]{:S(2)}) collective-permute-start(bf16[1,84,512]{2,1,0:T(8,128)(2,1)S(1)} %get-tuple-element.28.refs_1_), channel_id=1, source_target_pairs={{0,32},{32,0},{1,33},{33,1},{2,34},{34,2},{3,35},{35,3},{4,36},{36... | collective-permute-start | bytes 258056 | tf_op jit(solution)/shard_map/ppermute | solution.py:427
  31.5 13.6 %collective-permute-start.2 = (bf16[1,84,512]{2,1,0:T(8,128)(2,1)S(1)}, bf16[1,84,512]{2,1,0:T(8,128)(2,1)S(1)}, u32[]{:S(2)}, u32[]{:S(2)}) collective-permute-start(bf16[1,84,512]{2,1,0:T(8,128)(2,1)S(1)} %get-tuple-element.29.refs_2_), channel_id=1, source_target_pairs={{0,32},{32,0},{1,33},{33,1},{2,34},{34,2},{3,35},{35,3},{4,36},{36... | collective-permute-start | bytes 258056 | tf_op jit(solution)/shard_map/ppermute | solution.py:427

commit v3 on v2

--- a/solution.py
+++ b/solution.py
@@ -4,7 +4,6 @@
 import jax.numpy as jnp
 from jax import lax
 from jax.experimental import pallas as pl
-from jax.experimental.layout import Layout, with_layout_constraint
 from jax.experimental.pallas import tpu as pltpu
 from jax.sharding import PartitionSpec as P
 
@@ -16,7 +15,6 @@
 EPSILON = 1e-06
 LANES = 128
 GROUP = 4
-CHUNKS = (2, 1, 1)
 
 F32 = jnp.float32
 BF16 = jnp.bfloat16
@@ -62,21 +60,27 @@
     return counts
 
 
-def pool_kernel(enc_hbm, grid_hbm, pooled_ref, enc_ref, grid_ref, sems):
+def pool_kernel(enc_hbm, grid_hbm, noise_hbm, pooled_ref, enc_ref, grid_ref, noise_ref, sems):
     copies = [
         pltpu.make_async_copy(enc_hbm, enc_ref, sems.at[0]),
         pltpu.make_async_copy(grid_hbm, grid_ref, sems.at[1]),
+        pltpu.make_async_copy(noise_hbm, noise_ref, sems.at[2]),
     ]
     for copy in copies:
         copy.start()
     copies[0].wait()
     counts = counts_of(enc_ref[...], grid_ref.shape[1]).astype(BF16)
     copies[1].wait()
-    pooled_ref[...] = dot(grid_ref[...], counts) * (1.0 / K_ENC)
+    copies[2].wait()
+    v = grid_ref.shape[0]
+    pooled_ref[:v, :] = dot(grid_ref[...], counts) * (1.0 / K_ENC)
+    pooled_ref[v:, :] = jnp.zeros((pooled_ref.shape[0] - v, pooled_ref.shape[1]), F32)
+    members, nz = noise_ref.shape
+    pooled_ref[v : v + members, :nz] = noise_ref[...]
 
 
 def states_of(pooled, w_in):
-    values = pooled.T
+    values = pooled[: w_in.shape[0]].T
     high = values.astype(BF16)
     rest = values - high.astype(F32)
     mid = rest.astype(BF16)
@@ -88,6 +92,20 @@
     centre = states - jnp.mean(states, axis=-1, keepdims=True)
     spread = jnp.mean(centre * centre, axis=-1, keepdims=True)
     return centre / jnp.sqrt(spread + EPSILON)
+
+
+def conditioning(noise, w_gamma, w_beta):
+    gain = 1.0 + jnp.dot(noise, w_gamma, precision=lax.Precision.HIGHEST)
+    return gain, jnp.dot(noise, w_beta, precision=lax.Precision.HIGHEST)
+
+
+def project_into(out_ref, inputs, w_qkv_ref):
+    d = w_qkv_ref.shape[0]
+    for c in range(3):
+        part = dot(inputs, w_qkv_ref[:, c * d : (c + 1) * d])
+        if c == 0:
+            part = part * HD ** (-0.5)
+        out_ref[:, c * d : (c + 1) * d] = part.astype(BF16)
 
 
 def own_kernel(
@@ -105,10 +123,9 @@
     counts_ref,
     inputs_ref,
 ):
-    tok, d = states_ref.shape
+    tok, _ = states_ref.shape
     members = noise_ref.shape[0]
-    gain = 1.0 + jnp.dot(noise_ref[...], w_gamma_ref[...], precision=lax.Precision.HIGHEST)
-    shift = jnp.dot(noise_ref[...], w_beta_ref[...], precision=lax.Precision.HIGHEST)
+    gain, shift = conditioning(noise_ref[...], w_gamma_ref[...], w_beta_ref[...])
     gain_ref[...] = gain
     shift_ref[...] = shift
     states = states_of(pooled_ref[...], w_in_ref[...])
@@ -116,11 +133,7 @@
     normed = normed_of(states)
     for m in range(members):
         inputs_ref[m * tok : (m + 1) * tok, :] = (normed * gain[m : m + 1] + shift[m : m + 1]).astype(BF16)
-    for c in range(3):
-        part = dot(inputs_ref[...], w_qkv_ref[:, c * d : (c + 1) * d])
-        if c == 0:
-            part = part * HD ** (-0.5)
-        project_ref[:, c * d : (c + 1) * d] = part.astype(BF16)
+    project_into(project_ref, inputs_ref[...], w_qkv_ref)
     counts = counts_of(dec_ref[...], tok).T.astype(BF16)
     counts_ref[:, :tok] = counts
     counts_ref[:, tok:] = counts
@@ -128,10 +141,13 @@
 
 def members_kernel(
     begin,
+    own,
     nbr_ref,
     pair_ref,
     next_ref,
     w_in_ref,
+    w_gamma_ref,
+    w_beta_ref,
     gain_ref,
     shift_ref,
     project_ref,
@@ -143,11 +159,29 @@
     readout_ref,
     x_ref,
     feat_ref,
+    extra_ref,
     *refs,
 ):
-    edge_ref, kv_ref, att_ref, upd_ref = refs[-4:]
+    edge_ref, kv_ref, att_ref, upd_ref = refs[:4]
     tok, d = states_ref.shape
-    members = x_ref.shape[0]
+    members = kv_ref.shape[0]
+    gains = [gain_ref[begin + m : begin + m + 1, :] for m in range(own)]
+    shifts = [shift_ref[begin + m : begin + m + 1, :] for m in range(own)]
+    sources = [(project_ref, (begin + m) * tok) for m in range(own)]
+    if members > own:
+        mine_ref = refs[4]
+        v, count = w_in_ref.shape[0], gain_ref.shape[0]
+        noise = next_ref[v : v + count, : w_gamma_ref.shape[0]]
+        gain, shift = conditioning(noise, w_gamma_ref[...], w_beta_ref[...])
+        normed = normed_of(states_ref[...])
+        rows = []
+        for m in range(members - own):
+            k = begin + m
+            gains.append(gain[k : k + 1])
+            shifts.append(shift[k : k + 1])
+            sources.append((mine_ref, m * tok))
+            rows.append((normed * gains[-1] + shifts[-1]).astype(BF16))
+        project_into(mine_ref, jnp.concatenate(rows, axis=0), w_qkv_ref)
     wins = tok // WIN
     wide = GROUP * HD
     windows = wins * lax.axis_size("space")
@@ -157,23 +191,19 @@
         if begin == 0:
             pooled = jnp.where(odd == (slot == 0), pair_ref[...], next_ref[...])
             normed = normed_of(states_of(pooled, w_in_ref[...]))
-            refs[0][slot * tok : (slot + 1) * tok, :] = normed
+            extra_ref[slot * tok : (slot + 1) * tok, :] = normed
         else:
             normed = pair_ref[slot * tok : (slot + 1) * tok, :]
         for m in range(members):
             row = (2 * m + slot) * tok
-            k = begin + m
-            edge_ref[row : row + tok, :] = (
-                normed * gain_ref[k : k + 1, :] + shift_ref[k : k + 1, :]
-            ).astype(BF16)
+            edge_ref[row : row + tok, :] = (normed * gains[m] + shifts[m]).astype(BF16)
     for c in range(2):
         lo = c * d
         part = dot(edge_ref[...], w_qkv_ref[:, d + lo : d + lo + d]).astype(BF16)
         for m in range(members):
             kv_ref[m, :tok, lo : lo + d] = part[2 * m * tok : (2 * m + 1) * tok]
-            kv_ref[m, tok : 2 * tok, lo : lo + d] = project_ref[
-                (begin + m) * tok : (begin + m + 1) * tok, d + lo : d + lo + d
-            ]
+            ref, row = sources[m]
+            kv_ref[m, tok : 2 * tok, lo : lo + d] = ref[row : row + tok, d + lo : d + lo + d]
             kv_ref[m, 2 * tok :, lo : lo + d] = part[(2 * m + 1) * tok : (2 * m + 2) * tok]
     head_of = lax.broadcasted_iota(jnp.int32, (WIN, wide), 1) // HD
 
@@ -186,7 +216,8 @@
             row = m * tok + w * WIN
             for g in range(HEADS // GROUP):
                 lo = g * wide
-                q = project_ref[pl.ds(begin * tok + row, WIN), lo : lo + wide]
+                ref, base = sources[m]
+                q = ref[base + w * WIN : base + (w + 1) * WIN, lo : lo + wide]
                 zero = jnp.zeros_like(q)
                 spread = jnp.concatenate([jnp.where(head_of == h, q, zero) for h in range(GROUP)], axis=0)
                 keys = jnp.concatenate([kv_ref[m, pl.ds(s, WIN), lo : lo + wide] for s in starts], axis=0)
@@ -201,7 +232,7 @@
                 out = mixed[:WIN]
                 for h in range(1, GROUP):
                     out = jnp.where(head_of == h, mixed[h * WIN : (h + 1) * WIN], out)
-                att_ref[pl.ds(row, WIN), lo : lo + wide] = out.astype(BF16)
+                att_ref[row : row + WIN, lo : lo + wide] = out.astype(BF16)
 
     for m in range(members):
         attend(m)
@@ -212,13 +243,17 @@
         upd_ref[m, :tok, :] = high
         upd_ref[m, tok:, :] = (updated - high.astype(F32)).astype(BF16)
 
-    def decode(m, carry):
+    def decode(m, out_ref, slot, keep):
         features = (dot(counts_ref[...], upd_ref[m]) / K_DEC).astype(BF16)
-        feat_ref[m] = features
-        x_ref[m] = (grid_ref[...].astype(F32) + dot_nt(readout_ref[...], features)).astype(BF16)
-        return carry
-
-    lax.fori_loop(0, members, decode, 0)
+        if keep:
+            feat_ref[slot] = features
+        x = grid_ref[...].astype(F32) + dot_nt(readout_ref[...], features)
+        out_ref[slot] = x.astype(BF16)
+
+    for m in range(own):
+        decode(m, x_ref, m, True)
+    for m in range(own, members):
+        decode(m, extra_ref, m - own, False)
 
 
 def pair_list(own, other):
@@ -360,19 +395,20 @@
 
     pooled = call(
         pool_kernel,
-        pltpu.VMEM((v, tok), F32),
-        (enc_index.T, grid),
-        hbm=(0, 1),
+        pltpu.VMEM((v + members, tok), F32),
+        (enc_index.T, grid, noise[0]),
+        hbm=(0, 1, 2),
         scratch=(
             pltpu.VMEM((enc_index.shape[1], tok), jnp.int32),
             pltpu.VMEM((v, points), BF16),
-            pltpu.SemaphoreType.DMA((2,)),
+            pltpu.VMEM(noise.shape[1:], F32),
+            pltpu.SemaphoreType.DMA((3,)),
         ),
         work=4 * 10**9,
     )
-    pairs = [(i, i ^ 1) for i in range(space)]
+    pairs = [(q * space + i, (1 - q) * space + (i ^ 1)) for q in range(2) for i in range(space)]
     nexts = [(i, (i + 1 if i % 2 else i - 1) % space) for i in range(space)]
-    from_pair = lax.ppermute(pooled, "space", pairs)
+    from_pair = lax.ppermute(pooled, ("member", "space"), pairs)
     from_next = lax.ppermute(pooled, "space", nexts)
     states, gain, shift, project, counts = call(
         own_kernel,
@@ -387,20 +423,27 @@
         scratch=(pltpu.VMEM((members * tok, d), BF16),),
         work=4 * 10**9,
     )
-    own, other, feats = [], [], []
-    halo = (from_pair, from_next)
-    begin = 0
-    for some in CHUNKS:
-        outs = [pltpu.VMEM((some, v, points), BF16), pltpu.VMEM((some, points, d), BF16)]
-        if begin == 0:
-            outs.append(pltpu.VMEM((2 * tok, d), F32))
-        got = call(
-            functools.partial(members_kernel, begin),
-            outs,
+    half = members // 2
+    forecasts = pltpu.VMEM((half, v, points), BF16)
+
+    def run(begin, extra_out, halo, slots):
+        scratch = [
+            pltpu.VMEM((2 * slots * tok, d), BF16),
+            pltpu.VMEM((slots, 3 * tok, 2 * d), BF16),
+            pltpu.VMEM((slots * tok, d), BF16),
+            pltpu.VMEM((slots, 2 * tok, d), BF16),
+        ]
+        if slots > half:
+            scratch.append(pltpu.VMEM(((slots - half) * tok, 3 * d), BF16))
+        return call(
+            functools.partial(members_kernel, begin, half),
+            [forecasts, pltpu.VMEM((half, points, d), BF16), extra_out],
             (
                 neighbours,
                 *halo,
                 w_in,
+                w_gamma,
+                w_beta,
                 gain,
                 shift,
                 project,
@@ -412,24 +455,16 @@
                 readout_matrix,
             ),
             smem=(0,),
-            scratch=(
-                pltpu.VMEM((2 * some * tok, d), BF16),
-                pltpu.VMEM((some, 3 * tok, 2 * d), BF16),
-                pltpu.VMEM((some * tok, d), BF16),
-                pltpu.VMEM((some, 2 * tok, d), BF16),
-            ),
+            scratch=scratch,
+            limit=36,
             work=8 * 10**9,
         )
-        if begin == 0:
-            halo = (got[2], from_next)
-        own.append(got[0])
-        feats.append(got[1])
-        other.append(lax.ppermute(got[0], "member", [(0, 1), (1, 0)]))
-        begin += some
-    pred = jnp.concatenate([x.transpose(1, 0, 2) for x in own], axis=1)
-    pred = with_layout_constraint(pred, Layout(major_to_minor=(0, 1, 2)))
-    pred, other[-1] = lax.optimization_barrier((pred, other[-1]))
-    pred = pred.transpose(1, 0, 2)
+
+    x_a, feat_a, normed = run(0, pltpu.VMEM((2 * tok, d), F32), (from_pair, from_next), half)
+    got_a = lax.ppermute(x_a, "member", [(0, 1), (1, 0)])
+    x_b, feat_b, got_b = run(half, forecasts, (normed, from_pair), members)
+    own, other, feats = [x_a, x_b], [got_a, got_b], [feat_a, feat_b]
+    pred = jnp.concatenate(own, axis=0)
     members_all = members * lax.axis_size("member")
     stats = call(
         functools.partial(stats_kernel, members),

time: 93.2 us -> 88.7 us (0.952)
  blocking collectives: 44.9 us -> 33.8 us
  Pallas kernels: 19.6 us -> 23.8 us
  waiting for transfers between devices: 6.73 us -> 9.01 us
  other arithmetic: 1.31 us -> 0.04 us
    all_to_all x4 -> x3, blocking collectives: 44.9 us -> 33.8 us  [exchange(): return lax.all_to_all(blocks, axis, split_axis=0, concat_axis=0, tiled=True)]
    all_to_all x0 -> x1, waiting for transfers between devices: none -> 6.83 us  [exchange(): return lax.all_to_all(blocks, axis, split_axis=0, concat_axis=0, tiled=True)]
    all_to_all x0 -> x1, starting transfers between devices: none -> 5.33 us  [exchange(): return lax.all_to_all(blocks, axis, split_axis=0, concat_axis=0, tiled=True)]
    ppermute x4 -> x2, waiting for transfers between devices: 6.73 us -> 2.17 us  [the longest x1 2.17 us: step(): got_a = lax.ppermute(x_a, 'member', [(0, 1), (1, 0)])]
    ppermute x4 -> x2, starting transfers between devices: 16.2 us -> 11.7 us  [the longest x1 10.3 us: step(): from_pair = lax.ppermute(pooled, ('member', 'space'), pairs)]
    pallas_call x10 -> x9, Pallas kernels: 19.6 us -> 23.8 us  [call(): pl.pallas_call(kernel, out_shape=outs, in_specs=[SMEM if i in smem else H...]
    concatenate x1 -> x0, other arithmetic: 1.31 us -> none  [step(): pred = jnp.concatenate([x.transpose(1, 0, 2) for x in own], axis=1)]
  transfers between devices with their start and end apart: 5 -> 4, of which waited for: 1 -> 2; matrix products, arithmetic and copies ran while one was open for 2% -> 1% of each run, Pallas kernels for 10% -> 15%
where the time goes in v3:
time: 88.7 us; the launch traced here: 88.5 us
  blocking collectives  33.8 us (38%)
  Pallas kernels  23.8 us (27%)
  starting transfers between devices  19.8 us (22%)
  waiting for transfers between devices  9.01 us (10%)
  between operations  1 us (1%)
  local copies, waits for them, and re-layouts  0.96 us (1%)
    all_to_all x3, blocking collectives, exchange(): return lax.all_to_all(blocks, axis, split_axis=0, concat_axis=0, tiled=True)  33.8 us
    pallas_call x9, Pallas kernels, call(): pl.pallas_call(kernel, out_shape=outs, in_specs=[SMEM if i in smem else H...  23.8 us
    ppermute x1, starting transfers between devices, step(): from_pair = lax.ppermute(pooled, ('member', 'space'), pairs)  10.3 us
    all_to_all x1, waiting for transfers between devices, exchange(): return lax.all_to_all(blocks, axis, split_axis=0, concat_axis=0, tiled=True)  6.83 us
    all_to_all x1, starting transfers between devices, exchange(): return lax.all_to_all(blocks, axis, split_axis=0, concat_axis=0, tiled=True)  5.33 us
    ppermute x1, starting transfers between devices, step(): from_next = lax.ppermute(pooled, 'space', nexts)  2.76 us
    ppermute x1, waiting for transfers between devices, step(): got_a = lax.ppermute(x_a, 'member', [(0, 1), (1, 0)])  2.17 us
  transfers between devices with their start and end apart: 4, of which 2 were waited for; matrix products, arithmetic and copies ran while one was open for 1% of the time, Pallas kernels for 15%

profile of v3, /device:TPU:1, one launch (start us, length us, event | category | flops | bytes accessed | tf_op | source)
XLA Modules:
  0.0 88.5 jit_solution(3477690251130692146)
XLA Ops:
  0.6 0.0 copy-start.1
  0.6 0.0 copy-start.3
  0.7 0.0 copy-start.5
  0.7 0.0 copy-start.6
  0.7 0.0 copy-start.8
  0.7 0.0 copy-start.9
  0.7 1.2 %shard_map.139.pooled_ref = f32[88,128]{1,0:T(8,128)S(1)} custom-call(s32[4,128]{1,0:T(4,128)} %bitcast.16, bf16[84,512]{1,0:T(8,128)(2,1)} %bitcast.10, f32[4,32]{1,0:T(4,128)} %bitcast.14), custom_call_target="tpu_custom_call" | custom-call | flops 4000000000 | bytes 40000000 | tf_op jit(solution)/shard_map/pallas_call | solution.py:42
  2.0 2.8 %collective-permute-start.1 = (f32[88,128]{1,0:T(8,128)S(1)}, f32[88,128]{1,0:T(8,128)S(1)}, u32[]{:S(2)}, u32[]{:S(2)}) collective-permute-start(f32[88,128]{1,0:T(8,128)S(1)} %shard_map.139.pooled_ref), channel_id=1, source_target_pairs={{0,31},{1,2},{2,1},{3,4},{4,3},{5,6},{6,5},{7,8},{8,7},{9,10},{10,... | collective-permute-start | bytes 135176 | tf_op jit(solution)/shard_map/ppermute | solution.py:412
  4.7 10.3 %collective-permute-start = (f32[88,128]{1,0:T(8,128)S(1)}, f32[88,128]{1,0:T(8,128)S(1)}, u32[]{:S(2)}, u32[]{:S(2)}) collective-permute-start(f32[88,128]{1,0:T(8,128)S(1)} %shard_map.139.pooled_ref), channel_id=1, source_target_pairs={{0,33},{1,32},{2,35},{3,34},{4,37},{5,36},{6,39},{7,38},{8,41},{9,... | collective-permute-start | bytes 135176 | tf_op jit(solution)/shard_map/ppermute | solution.py:411
  15.0 0.0 copy-done.5
  15.0 0.0 copy-start.2
  15.0 0.0 copy-start.4
  15.0 0.0 copy-start.7
  15.0 0.0 copy-start.10
  15.1 2.7 %shard_map.140 = (f32[128,768]{1,0:T(8,128)S(1)}, f32[4,768]{1,0:T(4,128)S(1)}, f32[4,768]{1,0:T(4,128)S(1)}, bf16[512,2304]{1,0:T(8,128)(2,1)S(1)}, bf16[512,256]{1,0:T(8,128)(2,1)S(1)}) custom-call(f32[88,128]{1,0:T(8,128)S(1)} %shard_map.139.pooled_ref, bf16[84,768]{1,0:T(8,128)(2,1)S(1)} %copy-done.3, f32[4,32]{1,0:T(4,128)S(1)} %bitcast.15, ...), custom_call_target="tpu_custom_call" | custom-call | flops 4000000000 | bytes 40000000 | tf_op jit(solution)/shard_map/pallas_call | solution.py:42
  17.8 0.0 collective-permute-done.1.next_ref
  17.8 0.0 collective-permute-done.pair_ref.next_ref
  17.8 6.1 %shard_map.141 = (bf16[2,84,512]{2,1,0:T(8,128)(2,1)S(1)}, bf16[2,512,768]{2,1,0:T(8,128)(2,1)S(1)}, f32[256,768]{1,0:T(8,128)S(1)}) custom-call(s32[2,3]{1,0:T(2,128)S(1)} %copy-done.10, f32[88,128]{1,0:T(8,128)S(1)} %collective-permute-done.pair_ref.next_ref, f32[88,128]{1,0:T(8,128)S(1)} %collective-permute-done.1.next_ref, ...), custom_call_target="tpu_custom_call" | custom-call | flops 8000000000 | bytes 80000000 | tf_op jit(solution)/shard_map/pallas_call | solution.py:42
  23.9 1.5 %collective-permute-start.2 = (bf16[2,84,512]{2,1,0:T(8,128)(2,1)S(1)}, bf16[2,84,512]{2,1,0:T(8,128)(2,1)S(1)}, u32[]{:S(2)}, u32[]{:S(2)}) collective-permute-start(bf16[2,84,512]{2,1,0:T(8,128)(2,1)S(1)} %get-tuple-element.23.refs_0_), channel_id=1, source_target_pairs={{0,32},{32,0},{1,33},{33,1},{2,34},{34,2},{3,35},{35,3},{4,36},{36... | collective-permute-start | bytes 516104 | tf_op jit(solution)/shard_map/ppermute | solution.py:464
  25.4 10.2 %shard_map.142 = (bf16[2,84,512]{2,1,0:T(8,128)(2,1)S(1)}, bf16[2,512,768]{2,1,0:T(8,128)(2,1)S(1)}, bf16[2,84,512]{2,1,0:T(8,128)(2,1)S(1)}) custom-call(s32[2,3]{1,0:T(2,128)S(1)} %copy-done.10, f32[256,768]{1,0:T(8,128)S(1)} %get-tuple-element.24.pair_ref, f32[88,128]{1,0:T(8,128)S(1)} %collective-permute-done.pair_ref.next_ref, ...), custom_call_target="tpu_custom_call" | custom-call | flops 8000000000 | bytes 80000000 | tf_op jit(solution)/shard_map/pallas_call | solution.py:42
  35.6 2.2 %collective-permute-done.2.refs_2_ = bf16[2,84,512]{2,1,0:T(8,128)(2,1)S(1)} collective-permute-done((bf16[2,84,512]{2,1,0:T(8,128)(2,1)S(1)}, bf16[2,84,512]{2,1,0:T(8,128)(2,1)S(1)}, u32[]{:S(2)}, u32[]{:S(2)}) %collective-permute-start.2) | collective-permute-done | bytes 172064 | tf_op jit(solution)/shard_map/ppermute | solution.py:464
  37.8 0.0 copy-done
  37.8 0.8 shard_map.143
  38.6 11.7 %all_to_all.20.stat_ref = f32[32,1,128]{2,1,0:T(1,128)S(1)} all-to-all(f32[32,1,128]{2,1,0:T(1,128)S(1)} %shard_map.143), channel_id=1, replica_groups=mesh['dp'=4,'member'=2,'space'=32] {'space'}, dimensions={0} | all-to-all | bytes 32768 | tf_op jit(solution)/shard_map/all_to_all | solution.py:370
  50.3 1.1 %shard_map.144 = (bf16[32,16,128]{2,1,0:T(8,128)(2,1)S(1)}, f32[8,128]{1,0:T(8,128)S(1)}) custom-call(f32[32,1,128]{2,1,0:T(1,128)S(1)} %all_to_all.20.stat_ref, bf16[84,512]{1,0:T(8,128)(2,1)S(1)} %bitcast.9, bf16[2,84,512]{2,1,0:T(8,128)(2,1)S(1)} %get-tuple-element.23.refs_0_, bf16[2,84,512]{2,1,0:T(8,128)(2,1)S(1)} %get-tuple-element.25.refs_1_, ...), custom_call_target="tpu_custom_call" | custom-call | tf_op jit(solution)/shard_map/pallas_call | solution.py:42
  51.5 11.4 %all_to_all.21.recv_ref = bf16[32,16,128]{2,1,0:T(8,128)(2,1)S(1)} all-to-all(bf16[32,16,128]{2,1,0:T(8,128)(2,1)S(1)} %get-tuple-element.29), channel_id=1, replica_groups=mesh['dp'=4,'member'=2,'space'=32] {'space'}, dimensions={0} | all-to-all | bytes 262144 | tf_op jit(solution)/shard_map/all_to_all | solution.py:370
  62.9 10.7 %all_to_all.22.recv_ref = f32[8,16,128]{2,1,0:T(8,128)S(1)} all-to-all(f32[8,16,128]{2,1,0:T(8,128)S(1)} %shard_map.145), channel_id=1, replica_groups=mesh['dp'=4,'member'=2,'space'=32] {'dp','member'}, dimensions={0} | all-to-all | bytes 131072 | tf_op jit(solution)/shard_map/all_to_all | solution.py:370
  73.6 0.7 shard_map.146
  74.3 5.3 %all-to-all-start.3 = ((bf16[32,16,128]{2,1,0:T(8,128)(2,1)}), bf16[32,16,128]{2,1,0:T(8,128)(2,1)S(1)}, u32[]{:S(2)}, u32[]{:S(2)}) async-start(bf16[32,16,128]{2,1,0:T(8,128)(2,1)} %shard_map.146), calls=%async_computation.3 | async-start | bytes 262144 | tf_op jit(solution)/shard_map/all_to_all | solution.py:370
  79.7 0.9 %copy.15 = bf16[1,4,84,512]{3,1,2,0:T(4,128)(2,1)} copy(bf16[1,4,84,512]{3,2,1,0:T(8,128)(2,1)S(1)} %maximum_bitcast_fusion) | data formatting | bytes 688128
  80.6 6.8 %all-to-all-done.3.recv_ref = bf16[32,16,128]{2,1,0:T(8,128)(2,1)S(1)} async-done(((bf16[32,16,128]{2,1,0:T(8,128)(2,1)}), bf16[32,16,128]{2,1,0:T(8,128)(2,1)S(1)}, u32[]{:S(2)}, u32[]{:S(2)}) %all-to-all-start.3) | async-done | bytes 131104 | tf_op jit(solution)/shard_map/all_to_all | solution.py:370
  87.4 0.9 %shard_map.147 = (f32[84,768]{1,0:T(8,128)}, f32[1]{0:T(128)}) custom-call(bf16[32,16,128]{2,1,0:T(8,128)(2,1)S(1)} %all-to-all-done.3.recv_ref), custom_call_target="tpu_custom_call" | custom-call | tf_op jit(solution)/shard_map/pallas_call | solution.py:42
  (12 shorter events, 0.1 us)
Async XLA Ops:
  0.6 14.3 %copy-start.1 = (bf16[768,2304]{1,0:T(8,128)(2,1)S(1)}, bf16[768,2304]{1,0:T(8,128)(2,1)}, u32[]{:S(2)}) copy-start(bf16[768,2304]{1,0:T(8,128)(2,1)} %w_qkv_ref.5) | copy-start | bytes 10616836
  0.6 14.3 %copy-start.3 = (bf16[84,768]{1,0:T(8,128)(2,1)S(1)}, bf16[84,768]{1,0:T(8,128)(2,1)}, u32[]{:S(2)}) copy-start(bf16[84,768]{1,0:T(8,128)(2,1)} %w_in_ref.5) | copy-start | bytes 387076
  0.7 14.3 %copy-start.5 = (f32[32,768]{1,0:T(8,128)S(1)}, f32[32,768]{1,0:T(8,128)}, u32[]{:S(2)}) copy-start(f32[32,768]{1,0:T(8,128)} %w_gamma_ref.5) | copy-start | bytes 294916
  0.7 14.3 %copy-start.6 = (f32[32,768]{1,0:T(8,128)S(1)}, f32[32,768]{1,0:T(8,128)}, u32[]{:S(2)}) copy-start(f32[32,768]{1,0:T(8,128)} %w_beta_ref.5) | copy-start | bytes 294916
  0.7 14.3 %copy-start.8 = (s32[512,3]{0,1:T(4,128)S(1)}, s32[512,3]{0,1:T(4,128)}, u32[]{:S(2)}) copy-start(s32[512,3]{0,1:T(4,128)} %param.17) | copy-start | bytes 18436
  0.7 14.3 %copy-start.9 = (f32[1,4,32]{2,1,0:T(4,128)S(1)}, f32[1,4,32]{2,1,0:T(4,128)}, u32[]{:S(2)}) copy-start(f32[1,4,32]{2,1,0:T(4,128)} %param.14) | copy-start | bytes 1540
  2.0 15.8 %collective-permute-start.1 = (f32[88,128]{1,0:T(8,128)S(1)}, f32[88,128]{1,0:T(8,128)S(1)}, u32[]{:S(2)}, u32[]{:S(2)}) collective-permute-start(f32[88,128]{1,0:T(8,128)S(1)} %shard_map.139.pooled_ref), channel_id=1, source_target_pairs={{0,31},{1,2},{2,1},{3,4},{4,3},{5,6},{6,5},{7,8},{8,7},{9,10},{10,... | collective-permute-start | bytes 135176 | tf_op jit(solution)/shard_map/ppermute | solution.py:412
  4.7 13.1 %collective-permute-start = (f32[88,128]{1,0:T(8,128)S(1)}, f32[88,128]{1,0:T(8,128)S(1)}, u32[]{:S(2)}, u32[]{:S(2)}) collective-permute-start(f32[88,128]{1,0:T(8,128)S(1)} %shard_map.139.pooled_ref), channel_id=1, source_target_pairs={{0,33},{1,32},{2,35},{3,34},{4,37},{5,36},{6,39},{7,38},{8,41},{9,... | collective-permute-start | bytes 135176 | tf_op jit(solution)/shard_map/ppermute | solution.py:411
  15.0 2.8 %copy-start.2 = (bf16[768,768]{1,0:T(8,128)(2,1)S(1)}, bf16[768,768]{1,0:T(8,128)(2,1)}, u32[]{:S(2)}) copy-start(bf16[768,768]{1,0:T(8,128)(2,1)} %w_o_ref.3) | copy-start | bytes 3538948
  15.0 2.8 %copy-start.4 = (bf16[84,768]{1,0:T(8,128)(2,1)S(1)}, bf16[84,768]{1,0:T(8,128)(2,1)}, u32[]{:S(2)}) copy-start(bf16[84,768]{1,0:T(8,128)(2,1)} %readout_ref.3) | copy-start | bytes 387076
  15.0 2.8 %copy-start.7 = (bf16[1,84,512]{2,1,0:T(8,128)(2,1)S(1)}, bf16[1,84,512]{2,1,0:T(8,128)(2,1)}, u32[]{:S(2)}) copy-start(bf16[1,84,512]{2,1,0:T(8,128)(2,1)} %param.12) | copy-start | bytes 258052
  15.0 2.8 %copy-start.10 = (s32[2,3]{1,0:T(2,128)S(1)}, s32[2,3]{1,0:T(2,128)}, u32[]{:S(2)}) copy-start(s32[2,3]{1,0:T(2,128)} %nbr_ref.3) | copy-start | bytes 76
  23.9 13.9 %collective-permute-start.2 = (bf16[2,84,512]{2,1,0:T(8,128)(2,1)S(1)}, bf16[2,84,512]{2,1,0:T(8,128)(2,1)S(1)}, u32[]{:S(2)}, u32[]{:S(2)}) collective-permute-start(bf16[2,84,512]{2,1,0:T(8,128)(2,1)S(1)} %get-tuple-element.23.refs_0_), channel_id=1, source_target_pairs={{0,32},{32,0},{1,33},{33,1},{2,34},{34,2},{3,35},{35,3},{4,36},{36... | collective-permute-start | bytes 516104 | tf_op jit(solution)/shard_map/ppermute | solution.py:464
  25.4 12.4 %copy-start = (bf16[1,84,512]{2,1,0:T(8,128)(2,1)S(1)}, bf16[1,84,512]{2,1,0:T(8,128)(2,1)}, u32[]{:S(2)}) copy-start(bf16[1,84,512]{2,1,0:T(8,128)(2,1)} %param.13) | copy-start | bytes 258052
  74.3 13.1 %all-to-all-start.3 = ((bf16[32,16,128]{2,1,0:T(8,128)(2,1)}), bf16[32,16,128]{2,1,0:T(8,128)(2,1)S(1)}, u32[]{:S(2)}, u32[]{:S(2)}) async-start(bf16[32,16,128]{2,1,0:T(8,128)(2,1)} %shard_map.146), calls=%async_computation.3 | async-start | bytes 262144 | tf_op jit(solution)/shard_map/all_to_all | solution.py:370

commit v4 on v3

--- a/solution.py
+++ b/solution.py
@@ -14,7 +14,8 @@
 K_DEC = 3
 EPSILON = 1e-06
 LANES = 128
-GROUP = 4
+GROUP = (4, 2)
+PART = (2, 2)
 
 F32 = jnp.float32
 BF16 = jnp.bfloat16
@@ -162,98 +163,120 @@
     extra_ref,
     *refs,
 ):
-    edge_ref, kv_ref, att_ref, upd_ref = refs[:4]
     tok, d = states_ref.shape
-    members = kv_ref.shape[0]
+    parted = [refs[4 * i : 4 * i + 4] for i in range(len(refs) // 4)]
+    each = parted[0][1].shape[0]
+    members = each * len(parted)
+    wins = tok // WIN
+    group = GROUP[begin > 0]
+    wide = group * HD
+    windows = wins * lax.axis_size("space")
+    first = lax.axis_index("space") * wins
     gains = [gain_ref[begin + m : begin + m + 1, :] for m in range(own)]
     shifts = [shift_ref[begin + m : begin + m + 1, :] for m in range(own)]
     sources = [(project_ref, (begin + m) * tok) for m in range(own)]
     if members > own:
-        mine_ref = refs[4]
+        mine_ref = refs[-1]
         v, count = w_in_ref.shape[0], gain_ref.shape[0]
         noise = next_ref[v : v + count, : w_gamma_ref.shape[0]]
         gain, shift = conditioning(noise, w_gamma_ref[...], w_beta_ref[...])
-        normed = normed_of(states_ref[...])
-        rows = []
         for m in range(members - own):
             k = begin + m
             gains.append(gain[k : k + 1])
             shifts.append(shift[k : k + 1])
             sources.append((mine_ref, m * tok))
-            rows.append((normed * gains[-1] + shifts[-1]).astype(BF16))
-        project_into(mine_ref, jnp.concatenate(rows, axis=0), w_qkv_ref)
-    wins = tok // WIN
-    wide = GROUP * HD
-    windows = wins * lax.axis_size("space")
-    first = lax.axis_index("space") * wins
     odd = lax.rem(lax.axis_index("space"), 2) == 1
+    sides = []
     for slot in range(2):
         if begin == 0:
             pooled = jnp.where(odd == (slot == 0), pair_ref[...], next_ref[...])
-            normed = normed_of(states_of(pooled, w_in_ref[...]))
-            extra_ref[slot * tok : (slot + 1) * tok, :] = normed
+            sides.append(normed_of(states_of(pooled, w_in_ref[...])))
+            extra_ref[slot * tok : (slot + 1) * tok, :] = sides[-1]
         else:
-            normed = pair_ref[slot * tok : (slot + 1) * tok, :]
-        for m in range(members):
-            row = (2 * m + slot) * tok
-            edge_ref[row : row + tok, :] = (normed * gains[m] + shifts[m]).astype(BF16)
-    for c in range(2):
-        lo = c * d
-        part = dot(edge_ref[...], w_qkv_ref[:, d + lo : d + lo + d]).astype(BF16)
-        for m in range(members):
-            kv_ref[m, :tok, lo : lo + d] = part[2 * m * tok : (2 * m + 1) * tok]
-            ref, row = sources[m]
-            kv_ref[m, tok : 2 * tok, lo : lo + d] = ref[row : row + tok, d + lo : d + lo + d]
-            kv_ref[m, 2 * tok :, lo : lo + d] = part[(2 * m + 1) * tok : (2 * m + 2) * tok]
+            sides.append(pair_ref[slot * tok : (slot + 1) * tok, :])
     head_of = lax.broadcasted_iota(jnp.int32, (WIN, wide), 1) // HD
-
-    def attend(m):
-        for w in range(wins):
-            starts = [(wins + w) * WIN]
-            for j in range(nbr_ref.shape[1]):
-                reach = lax.rem(nbr_ref[w, j] - first - w + 2 + windows, windows) + w
-                starts.append(pl.multiple_of(reach * WIN, WIN))
-            row = m * tok + w * WIN
-            for g in range(HEADS // GROUP):
-                lo = g * wide
-                ref, base = sources[m]
-                q = ref[base + w * WIN : base + (w + 1) * WIN, lo : lo + wide]
-                zero = jnp.zeros_like(q)
-                spread = jnp.concatenate([jnp.where(head_of == h, q, zero) for h in range(GROUP)], axis=0)
-                keys = jnp.concatenate([kv_ref[m, pl.ds(s, WIN), lo : lo + wide] for s in starts], axis=0)
-                values = jnp.concatenate(
-                    [kv_ref[m, pl.ds(s, WIN), d + lo : d + lo + wide] for s in starts], axis=0
-                )
-                scores = dot_nt(spread, keys)
-                top = jnp.max(scores, axis=-1, keepdims=True)
-                weights = jnp.exp(scores - top)
-                weights = weights * (1.0 / jnp.sum(weights, axis=-1, keepdims=True))
-                mixed = dot(weights.astype(BF16), values)
-                out = mixed[:WIN]
-                for h in range(1, GROUP):
-                    out = jnp.where(head_of == h, mixed[h * WIN : (h + 1) * WIN], out)
-                att_ref[row : row + WIN, lo : lo + wide] = out.astype(BF16)
-
-    for m in range(members):
-        attend(m)
-    mixed = dot(att_ref[...], w_o_ref[...])
-    for m in range(members):
-        updated = states_ref[...] + mixed[m * tok : (m + 1) * tok]
-        high = updated.astype(BF16)
-        upd_ref[m, :tok, :] = high
-        upd_ref[m, tok:, :] = (updated - high.astype(F32)).astype(BF16)
-
-    def decode(m, out_ref, slot, keep):
-        features = (dot(counts_ref[...], upd_ref[m]) / K_DEC).astype(BF16)
-        if keep:
-            feat_ref[slot] = features
-        x = grid_ref[...].astype(F32) + dot_nt(readout_ref[...], features)
-        out_ref[slot] = x.astype(BF16)
-
-    for m in range(own):
-        decode(m, x_ref, m, True)
-    for m in range(own, members):
-        decode(m, extra_ref, m - own, False)
+    starts = []
+    for w in range(wins):
+        starts.append([(wins + w) * WIN])
+        for j in range(nbr_ref.shape[1]):
+            reach = lax.rem(nbr_ref[w, j] - first - w + 2 + windows, windows) + w
+            starts[w].append(pl.multiple_of(reach * WIN, WIN))
+
+    def project(p):
+        edge_ref, kv_ref, _, _ = parted[p]
+        if p * each >= own:
+            normed = normed_of(states_ref[...])
+            ms = range(p * each, (p + 1) * each)
+            rows = [(normed * gains[m] + shifts[m]).astype(BF16) for m in ms]
+            lo = (p * each - own) * tok
+            project_into(mine_ref.at[lo : lo + each * tok], jnp.concatenate(rows, axis=0), w_qkv_ref)
+        for m in range(each):
+            k = p * each + m
+            for slot in range(2):
+                row = (2 * m + slot) * tok
+                edge_ref[row : row + tok, :] = (sides[slot] * gains[k] + shifts[k]).astype(BF16)
+        for c in range(2):
+            lo = c * d
+            part = dot(edge_ref[...], w_qkv_ref[:, d + lo : d + lo + d]).astype(BF16)
+            for m in range(each):
+                kv_ref[m, :tok, lo : lo + d] = part[2 * m * tok : (2 * m + 1) * tok]
+                ref, row = sources[p * each + m]
+                kv_ref[m, tok : 2 * tok, lo : lo + d] = ref[row : row + tok, d + lo : d + lo + d]
+                kv_ref[m, 2 * tok :, lo : lo + d] = part[(2 * m + 1) * tok : (2 * m + 2) * tok]
+
+    def attend(p):
+        _, kv_ref, att_ref, _ = parted[p]
+        for m in range(each):
+            ref, base = sources[p * each + m]
+            for w in range(wins):
+                row = m * tok + w * WIN
+                for g in range(HEADS // group):
+                    lo = g * wide
+                    q = ref[base + w * WIN : base + (w + 1) * WIN, lo : lo + wide]
+                    zero = jnp.zeros_like(q)
+                    spread = jnp.concatenate(
+                        [jnp.where(head_of == h, q, zero) for h in range(group)], axis=0
+                    )
+                    keys = jnp.concatenate(
+                        [kv_ref[m, pl.ds(s, WIN), lo : lo + wide] for s in starts[w]], axis=0
+                    )
+                    values = jnp.concatenate(
+                        [kv_ref[m, pl.ds(s, WIN), d + lo : d + lo + wide] for s in starts[w]], axis=0
+                    )
+                    scores = dot_nt(spread, keys)
+                    top = jnp.max(scores, axis=-1, keepdims=True)
+                    weights = jnp.exp(scores - top)
+                    weights = weights * (1.0 / jnp.sum(weights, axis=-1, keepdims=True))
+                    mixed = dot(weights.astype(BF16), values)
+                    out = mixed[:WIN]
+                    for h in range(1, group):
+                        out = jnp.where(head_of == h, mixed[h * WIN : (h + 1) * WIN], out)
+                    att_ref[row : row + WIN, lo : lo + wide] = out.astype(BF16)
+
+    def decode(p):
+        _, _, att_ref, upd_ref = parted[p]
+        mixed = dot(att_ref[...], w_o_ref[...])
+        for m in range(each):
+            updated = (states_ref[...] + mixed[m * tok : (m + 1) * tok]) * (1.0 / K_DEC)
+            high = updated.astype(BF16)
+            upd_ref[m, :tok, :] = high
+            upd_ref[m, tok:, :] = (updated - high.astype(F32)).astype(BF16)
+        for m in range(each):
+            k = p * each + m
+            features = dot(counts_ref[...], upd_ref[m]).astype(BF16)
+            x = grid_ref[...].astype(F32) + dot_nt(readout_ref[...], features)
+            if k < own:
+                feat_ref[k] = features
+                x_ref[k] = x.astype(BF16)
+            else:
+                extra_ref[k - own] = x.astype(BF16)
+
+    project(0)
+    for p in range(len(parted)):
+        attend(p)
+        if p + 1 < len(parted):
+            project(p + 1)
+        decode(p)
 
 
 def pair_list(own, other):
@@ -427,12 +450,13 @@
     forecasts = pltpu.VMEM((half, v, points), BF16)
 
     def run(begin, extra_out, halo, slots):
+        each = PART[begin > 0]
         scratch = [
-            pltpu.VMEM((2 * slots * tok, d), BF16),
-            pltpu.VMEM((slots, 3 * tok, 2 * d), BF16),
-            pltpu.VMEM((slots * tok, d), BF16),
-            pltpu.VMEM((slots, 2 * tok, d), BF16),
-        ]
+            pltpu.VMEM((2 * each * tok, d), BF16),
+            pltpu.VMEM((each, 3 * tok, 2 * d), BF16),
+            pltpu.VMEM((each * tok, d), BF16),
+            pltpu.VMEM((each, 2 * tok, d), BF16),
+        ] * (slots // each)
         if slots > half:
             scratch.append(pltpu.VMEM(((slots - half) * tok, 3 * d), BF16))
         return call(

time: 88.7 us -> 88.7 us (level)
  transfers between devices with their start and end apart: 4 -> 4, of which waited for: 2 -> 2; matrix products, arithmetic and copies ran while one was open for 1% -> 1% of each run, Pallas kernels for 15% -> 14%
where the time goes in v4:
time: 88.7 us; the launch traced here: 88.5 us
  blocking collectives  33.8 us (38%)
  Pallas kernels  23.5 us (26%)
  starting transfers between devices  19.8 us (22%)
  waiting for transfers between devices  9.34 us (11%)
  between operations  1 us (1%)
  local copies, waits for them, and re-layouts  0.96 us (1%)
    all_to_all x3, blocking collectives, exchange(): return lax.all_to_all(blocks, axis, split_axis=0, concat_axis=0, tiled=True)  33.8 us
    pallas_call x9, Pallas kernels, call(): pl.pallas_call(kernel, out_shape=outs, in_specs=[SMEM if i in smem else H...  23.5 us
    ppermute x1, starting transfers between devices, step(): from_pair = lax.ppermute(pooled, ('member', 'space'), pairs)  10.3 us
    all_to_all x1, waiting for transfers between devices, exchange(): return lax.all_to_all(blocks, axis, split_axis=0, concat_axis=0, tiled=True)  6.83 us
    all_to_all x1, starting transfers between devices, exchange(): return lax.all_to_all(blocks, axis, split_axis=0, concat_axis=0, tiled=True)  5.33 us
    ppermute x1, starting transfers between devices, step(): from_next = lax.ppermute(pooled, 'space', nexts)  2.76 us
    ppermute x1, waiting for transfers between devices, step(): got_a = lax.ppermute(x_a, 'member', [(0, 1), (1, 0)])  2.5 us
  transfers between devices with their start and end apart: 4, of which 2 were waited for; matrix products, arithmetic and copies ran while one was open for 1% of the time, Pallas kernels for 14%

profile of v4, /device:TPU:1, one launch (start us, length us, event | category | flops | bytes accessed | tf_op | source)
XLA Modules:
  0.0 88.5 jit_solution(8367717053376676356)
XLA Ops:
  0.6 0.0 copy-start.1
  0.6 0.0 copy-start.3
  0.7 0.0 copy-start.5
  0.7 0.0 copy-start.6
  0.7 0.0 copy-start.8
  0.7 0.0 copy-start.9
  0.7 1.2 %shard_map.139.pooled_ref = f32[88,128]{1,0:T(8,128)S(1)} custom-call(s32[4,128]{1,0:T(4,128)} %bitcast.16, bf16[84,512]{1,0:T(8,128)(2,1)} %bitcast.10, f32[4,32]{1,0:T(4,128)} %bitcast.14), custom_call_target="tpu_custom_call" | custom-call | flops 4000000000 | bytes 40000000 | tf_op jit(solution)/shard_map/pallas_call | solution.py:43
  2.0 2.8 %collective-permute-start.1 = (f32[88,128]{1,0:T(8,128)S(1)}, f32[88,128]{1,0:T(8,128)S(1)}, u32[]{:S(2)}, u32[]{:S(2)}) collective-permute-start(f32[88,128]{1,0:T(8,128)S(1)} %shard_map.139.pooled_ref), channel_id=1, source_target_pairs={{0,31},{1,2},{2,1},{3,4},{4,3},{5,6},{6,5},{7,8},{8,7},{9,10},{10,... | collective-permute-start | bytes 135176 | tf_op jit(solution)/shard_map/ppermute | solution.py:435
  4.7 10.3 %collective-permute-start = (f32[88,128]{1,0:T(8,128)S(1)}, f32[88,128]{1,0:T(8,128)S(1)}, u32[]{:S(2)}, u32[]{:S(2)}) collective-permute-start(f32[88,128]{1,0:T(8,128)S(1)} %shard_map.139.pooled_ref), channel_id=1, source_target_pairs={{0,33},{1,32},{2,35},{3,34},{4,37},{5,36},{6,39},{7,38},{8,41},{9,... | collective-permute-start | bytes 135176 | tf_op jit(solution)/shard_map/ppermute | solution.py:434
  15.0 0.0 copy-done.1
  15.0 0.0 copy-done.5
  15.0 0.0 copy-start.2
  15.0 0.0 copy-start.4
  15.0 0.0 copy-start.7
  15.0 0.0 copy-start.10
  15.1 2.7 %shard_map.140 = (f32[128,768]{1,0:T(8,128)S(1)}, f32[4,768]{1,0:T(4,128)S(1)}, f32[4,768]{1,0:T(4,128)S(1)}, bf16[512,2304]{1,0:T(8,128)(2,1)S(1)}, bf16[512,256]{1,0:T(8,128)(2,1)S(1)}) custom-call(f32[88,128]{1,0:T(8,128)S(1)} %shard_map.139.pooled_ref, bf16[84,768]{1,0:T(8,128)(2,1)S(1)} %copy-done.3, f32[4,32]{1,0:T(4,128)S(1)} %bitcast.15, ...), custom_call_target="tpu_custom_call" | custom-call | flops 4000000000 | bytes 40000000 | tf_op jit(solution)/shard_map/pallas_call | solution.py:43
  17.8 0.0 collective-permute-done.1.next_ref
  17.8 0.0 collective-permute-done.pair_ref.next_ref
  17.8 6.1 %shard_map.141 = (bf16[2,84,512]{2,1,0:T(8,128)(2,1)S(1)}, bf16[2,512,768]{2,1,0:T(8,128)(2,1)S(1)}, f32[256,768]{1,0:T(8,128)S(1)}) custom-call(s32[2,3]{1,0:T(2,128)S(1)} %copy-done.10, f32[88,128]{1,0:T(8,128)S(1)} %collective-permute-done.pair_ref.next_ref, f32[88,128]{1,0:T(8,128)S(1)} %collective-permute-done.1.next_ref, ...), custom_call_target="tpu_custom_call" | custom-call | flops 8000000000 | bytes 80000000 | tf_op jit(solution)/shard_map/pallas_call | solution.py:43
  23.9 1.5 %collective-permute-start.2 = (bf16[2,84,512]{2,1,0:T(8,128)(2,1)S(1)}, bf16[2,84,512]{2,1,0:T(8,128)(2,1)S(1)}, u32[]{:S(2)}, u32[]{:S(2)}) collective-permute-start(bf16[2,84,512]{2,1,0:T(8,128)(2,1)S(1)} %get-tuple-element.23.refs_0_), channel_id=1, source_target_pairs={{0,32},{32,0},{1,33},{33,1},{2,34},{34,2},{3,35},{35,3},{4,36},{36... | collective-permute-start | bytes 516104 | tf_op jit(solution)/shard_map/ppermute | solution.py:488
  25.4 9.9 %shard_map.142 = (bf16[2,84,512]{2,1,0:T(8,128)(2,1)S(1)}, bf16[2,512,768]{2,1,0:T(8,128)(2,1)S(1)}, bf16[2,84,512]{2,1,0:T(8,128)(2,1)S(1)}) custom-call(s32[2,3]{1,0:T(2,128)S(1)} %copy-done.10, f32[256,768]{1,0:T(8,128)S(1)} %get-tuple-element.24.pair_ref, f32[88,128]{1,0:T(8,128)S(1)} %collective-permute-done.pair_ref.next_ref, ...), custom_call_target="tpu_custom_call" | custom-call | flops 8000000000 | bytes 80000000 | tf_op jit(solution)/shard_map/pallas_call | solution.py:43
  35.3 2.5 %collective-permute-done.2.refs_2_ = bf16[2,84,512]{2,1,0:T(8,128)(2,1)S(1)} collective-permute-done((bf16[2,84,512]{2,1,0:T(8,128)(2,1)S(1)}, bf16[2,84,512]{2,1,0:T(8,128)(2,1)S(1)}, u32[]{:S(2)}, u32[]{:S(2)}) %collective-permute-start.2) | collective-permute-done | bytes 172064 | tf_op jit(solution)/shard_map/ppermute | solution.py:488
  37.8 0.8 shard_map.143
  38.6 11.4 %all_to_all.20.stat_ref = f32[32,1,128]{2,1,0:T(1,128)S(1)} all-to-all(f32[32,1,128]{2,1,0:T(1,128)S(1)} %shard_map.143), channel_id=1, replica_groups=mesh['dp'=4,'member'=2,'space'=32] {'space'}, dimensions={0} | all-to-all | bytes 32768 | tf_op jit(solution)/shard_map/all_to_all | solution.py:393
  50.0 1.1 %shard_map.144 = (bf16[32,16,128]{2,1,0:T(8,128)(2,1)S(1)}, f32[8,128]{1,0:T(8,128)S(1)}) custom-call(f32[32,1,128]{2,1,0:T(1,128)S(1)} %all_to_all.20.stat_ref, bf16[84,512]{1,0:T(8,128)(2,1)S(1)} %bitcast.9, bf16[2,84,512]{2,1,0:T(8,128)(2,1)S(1)} %get-tuple-element.23.refs_0_, bf16[2,84,512]{2,1,0:T(8,128)(2,1)S(1)} %get-tuple-element.25.refs_1_, ...), custom_call_target="tpu_custom_call" | custom-call | tf_op jit(solution)/shard_map/pallas_call | solution.py:43
  51.1 11.4 %all_to_all.21.recv_ref = bf16[32,16,128]{2,1,0:T(8,128)(2,1)S(1)} all-to-all(bf16[32,16,128]{2,1,0:T(8,128)(2,1)S(1)} %get-tuple-element.29), channel_id=1, replica_groups=mesh['dp'=4,'member'=2,'space'=32] {'space'}, dimensions={0} | all-to-all | bytes 262144 | tf_op jit(solution)/shard_map/all_to_all | solution.py:393
  62.6 11.0 %all_to_all.22.recv_ref = f32[8,16,128]{2,1,0:T(8,128)S(1)} all-to-all(f32[8,16,128]{2,1,0:T(8,128)S(1)} %shard_map.145), channel_id=1, replica_groups=mesh['dp'=4,'member'=2,'space'=32] {'dp','member'}, dimensions={0} | all-to-all | bytes 131072 | tf_op jit(solution)/shard_map/all_to_all | solution.py:393
  73.6 0.7 shard_map.146
  74.3 5.3 %all-to-all-start.3 = ((bf16[32,16,128]{2,1,0:T(8,128)(2,1)}), bf16[32,16,128]{2,1,0:T(8,128)(2,1)S(1)}, u32[]{:S(2)}, u32[]{:S(2)}) async-start(bf16[32,16,128]{2,1,0:T(8,128)(2,1)} %shard_map.146), calls=%async_computation.3 | async-start | bytes 262144 | tf_op jit(solution)/shard_map/all_to_all | solution.py:393
  79.7 0.9 %copy.15 = bf16[1,4,84,512]{3,1,2,0:T(4,128)(2,1)} copy(bf16[1,4,84,512]{3,2,1,0:T(8,128)(2,1)S(1)} %maximum_bitcast_fusion) | data formatting | bytes 688128
  80.6 6.8 %all-to-all-done.3.recv_ref = bf16[32,16,128]{2,1,0:T(8,128)(2,1)S(1)} async-done(((bf16[32,16,128]{2,1,0:T(8,128)(2,1)}), bf16[32,16,128]{2,1,0:T(8,128)(2,1)S(1)}, u32[]{:S(2)}, u32[]{:S(2)}) %all-to-all-start.3) | async-done | bytes 131104 | tf_op jit(solution)/shard_map/all_to_all | solution.py:393
  87.4 0.9 %shard_map.147 = (f32[84,768]{1,0:T(8,128)}, f32[1]{0:T(128)}) custom-call(bf16[32,16,128]{2,1,0:T(8,128)(2,1)S(1)} %all-to-all-done.3.recv_ref), custom_call_target="tpu_custom_call" | custom-call | tf_op jit(solution)/shard_map/pallas_call | solution.py:43
  (12 shorter events, 0.1 us)
Async XLA Ops:
  0.6 14.3 %copy-start.1 = (bf16[768,2304]{1,0:T(8,128)(2,1)S(1)}, bf16[768,2304]{1,0:T(8,128)(2,1)}, u32[]{:S(2)}) copy-start(bf16[768,2304]{1,0:T(8,128)(2,1)} %w_qkv_ref.5) | copy-start | bytes 10616836
  0.6 14.3 %copy-start.3 = (bf16[84,768]{1,0:T(8,128)(2,1)S(1)}, bf16[84,768]{1,0:T(8,128)(2,1)}, u32[]{:S(2)}) copy-start(bf16[84,768]{1,0:T(8,128)(2,1)} %w_in_ref.5) | copy-start | bytes 387076
  0.7 14.3 %copy-start.5 = (f32[32,768]{1,0:T(8,128)S(1)}, f32[32,768]{1,0:T(8,128)}, u32[]{:S(2)}) copy-start(f32[32,768]{1,0:T(8,128)} %w_gamma_ref.5) | copy-start | bytes 294916
  0.7 14.3 %copy-start.6 = (f32[32,768]{1,0:T(8,128)S(1)}, f32[32,768]{1,0:T(8,128)}, u32[]{:S(2)}) copy-start(f32[32,768]{1,0:T(8,128)} %w_beta_ref.5) | copy-start | bytes 294916
  0.7 14.3 %copy-start.8 = (s32[512,3]{0,1:T(4,128)S(1)}, s32[512,3]{0,1:T(4,128)}, u32[]{:S(2)}) copy-start(s32[512,3]{0,1:T(4,128)} %param.17) | copy-start | bytes 18436
  0.7 14.3 %copy-start.9 = (f32[1,4,32]{2,1,0:T(4,128)S(1)}, f32[1,4,32]{2,1,0:T(4,128)}, u32[]{:S(2)}) copy-start(f32[1,4,32]{2,1,0:T(4,128)} %param.14) | copy-start | bytes 1540
  2.0 15.8 %collective-permute-start.1 = (f32[88,128]{1,0:T(8,128)S(1)}, f32[88,128]{1,0:T(8,128)S(1)}, u32[]{:S(2)}, u32[]{:S(2)}) collective-permute-start(f32[88,128]{1,0:T(8,128)S(1)} %shard_map.139.pooled_ref), channel_id=1, source_target_pairs={{0,31},{1,2},{2,1},{3,4},{4,3},{5,6},{6,5},{7,8},{8,7},{9,10},{10,... | collective-permute-start | bytes 135176 | tf_op jit(solution)/shard_map/ppermute | solution.py:435
  4.7 13.1 %collective-permute-start = (f32[88,128]{1,0:T(8,128)S(1)}, f32[88,128]{1,0:T(8,128)S(1)}, u32[]{:S(2)}, u32[]{:S(2)}) collective-permute-start(f32[88,128]{1,0:T(8,128)S(1)} %shard_map.139.pooled_ref), channel_id=1, source_target_pairs={{0,33},{1,32},{2,35},{3,34},{4,37},{5,36},{6,39},{7,38},{8,41},{9,... | collective-permute-start | bytes 135176 | tf_op jit(solution)/shard_map/ppermute | solution.py:434
  15.0 2.8 %copy-start.2 = (bf16[768,768]{1,0:T(8,128)(2,1)S(1)}, bf16[768,768]{1,0:T(8,128)(2,1)}, u32[]{:S(2)}) copy-start(bf16[768,768]{1,0:T(8,128)(2,1)} %w_o_ref.3) | copy-start | bytes 3538948
  15.0 2.8 %copy-start.4 = (bf16[84,768]{1,0:T(8,128)(2,1)S(1)}, bf16[84,768]{1,0:T(8,128)(2,1)}, u32[]{:S(2)}) copy-start(bf16[84,768]{1,0:T(8,128)(2,1)} %readout_ref.3) | copy-start | bytes 387076
  15.0 2.8 %copy-start.7 = (bf16[1,84,512]{2,1,0:T(8,128)(2,1)S(1)}, bf16[1,84,512]{2,1,0:T(8,128)(2,1)}, u32[]{:S(2)}) copy-start(bf16[1,84,512]{2,1,0:T(8,128)(2,1)} %param.12) | copy-start | bytes 258052
  15.0 2.8 %copy-start.10 = (s32[2,3]{1,0:T(2,128)S(1)}, s32[2,3]{1,0:T(2,128)}, u32[]{:S(2)}) copy-start(s32[2,3]{1,0:T(2,128)} %nbr_ref.3) | copy-start | bytes 76
  23.9 13.9 %collective-permute-start.2 = (bf16[2,84,512]{2,1,0:T(8,128)(2,1)S(1)}, bf16[2,84,512]{2,1,0:T(8,128)(2,1)S(1)}, u32[]{:S(2)}, u32[]{:S(2)}) collective-permute-start(bf16[2,84,512]{2,1,0:T(8,128)(2,1)S(1)} %get-tuple-element.23.refs_0_), channel_id=1, source_target_pairs={{0,32},{32,0},{1,33},{33,1},{2,34},{34,2},{3,35},{35,3},{4,36},{36... | collective-permute-start | bytes 516104 | tf_op jit(solution)/shard_map/ppermute | solution.py:488
  25.4 12.4 %copy-start = (bf16[1,84,512]{2,1,0:T(8,128)(2,1)S(1)}, bf16[1,84,512]{2,1,0:T(8,128)(2,1)}, u32[]{:S(2)}) copy-start(bf16[1,84,512]{2,1,0:T(8,128)(2,1)} %param.13) | copy-start | bytes 258052
  74.3 13.1 %all-to-all-start.3 = ((bf16[32,16,128]{2,1,0:T(8,128)(2,1)}), bf16[32,16,128]{2,1,0:T(8,128)(2,1)S(1)}, u32[]{:S(2)}, u32[]{:S(2)}) async-start(bf16[32,16,128]{2,1,0:T(8,128)(2,1)} %shard_map.146), calls=%async_computation.3 | async-start | bytes 262144 | tf_op jit(solution)/shard_map/all_to_all | solution.py:393
